TPU v7x, 128 devices: a whole 4x4x4 slice. The times are simulated.
128 devices in a mesh: dp: 16 (over y_hi, z, core), cache: 8 (over y_lo, x).
Axes of the slice: x: 4, y: 4 (y_hi: 2, y_lo: 2; y = y_hi * 2 + y_lo), z: 4, core: 2. Of those that a mesh axis runs over, the one named last changes fastest.
Arguments:
- hidden_in: bfloat16 [16384, 2560], P(('dp', 'cache')), may hold values from -6 to 6
- placing: int32 [16384], P('dp'), may hold values from 0 to 16383, as said below
- prompt_start: int32 [16384], P(('dp', 'cache')), may hold values from 0 to 16383, as said below
- attn_gain: float32 [2560], replicated, may hold values from 0.5 to 1.5
- w_qkv: bfloat16 [2560, 1792], P(('dp', 'cache'))
- w_out: bfloat16 [1280, 2560], P(('dp', 'cache')), may hold values from -0.15625 to 0.15625
- moe_gain: float32 [2560], replicated, may hold values from 0.5 to 1.5
- routes: int32 [16384, 6], P(('dp', 'cache')), may hold values from 0 to 63, all different within a row; in each aligned block of 128 rows (0 to 127, 128 to 255, ...) at most 16 rows name the same one
- route_weight: float32 [16384, 6], P(('dp', 'cache')), may hold values from 0.05 to 0.35
- w_gate_up: bfloat16 [128, 2560, 1536], P(('dp', 'cache')), may hold values from -0.125 to 0.125
- w_down: bfloat16 [128, 768, 2560], P(('dp', 'cache')), may hold values from -0.15625 to 0.15625
Outputs:
- mixed: bfloat16 [16384, 2560], P(('dp', 'cache'))
- cache_keys: bfloat16 [16384, 256], P(('dp', 'cache'))
- cache_values: bfloat16 [16384, 256], P(('dp', 'cache'))
Inputs may be any that keep to these rules, and one draw needn't show every extreme that they name: `placing`: a permutation of the 16384 positions; dealt rows g * 1024 to (g+1) * 1024 - 1 hold natural positions of the same range, and the dealt rows c * 128 + j * 16 to c * 128 + (j+1) * 16 - 1 of a group hold natural positions of its span j * 128 to (j+1) * 128 - 1. Prompts are runs of consecutive natural positions inside one group of 1024, of at most 512 tokens, some of exactly 512; prompt_start[r] <= placing[r] and it is the first position of that run. `routes`: in the rows of one device (aligned blocks of 128 rows) no expert is named more than 16 times.
All inputs are finite; a program needn't handle non-finite values.
Results may differ from a plain program's by a relative error of at most 0.014.
Values may be sent and summed in bfloat16 or wider, within the bound.
No kernel may reach another device: no remote copies, remote signals or barrier semaphores. Data moves between devices by JAX's collectives and lax.ppermute only.
A program may use at most 128 MiB of HBM per device.

v0:
```python
import jax
import jax.numpy as jnp
import numpy as np
from jax import lax
from jax.experimental import pallas as pl
from jax.experimental.pallas import tpu as pltpu
from jax.sharding import Mesh
from jax.sharding import PartitionSpec as P

HD = 128
QH = 10
KVH = 2
TOP = 6
MOST = 16

DP = ("yh", "z", "core")
CACHE = ("yl", "x")
SIZES = {"yh": 2, "z": 4, "core": 2, "yl": 2, "x": 4}
ALL = DP + CACHE
CHIPS = ("yh", "z", "yl", "x")
CHIP_COUNT = 64

norm_eps = 1e-05
rope_base = 500000.0
masked_score = -1e30


def linear(yh, z, core, yl, x):
    return (((yh * 4 + z) * 2 + core) * 2 + yl) * 4 + x


def swap_pairs():
    pairs = []
    for yh in range(2):
        for z in range(4):
            for yl in range(2):
                for x in range(0, 4, 2):
                    low = linear(yh, z, 1, yl, x)
                    high = linear(yh, z, 0, yl, x + 1)
                    pairs += [(low, high), (high, low)]
    return pairs


def rms_scaled(features, gain_vector):
    widened = features.astype(jnp.float32)
    factor = lax.rsqrt(jnp.mean(widened * widened, axis=-1, keepdims=True) + norm_eps)
    return (widened * factor * gain_vector).astype(jnp.bfloat16)


def rotated(grouped, cosine, sine_part):
    half_size = HD // 2
    first_half = grouped[..., :half_size]
    second = grouped[..., half_size:]
    return jnp.concatenate(
        [first_half * cosine - second * sine_part, second * cosine + first_half * sine_part],
        axis=-1,
    ).astype(jnp.bfloat16)


def spread(shard, axes, count):
    return lax.all_to_all(
        jnp.broadcast_to(shard[None], (count,) + shard.shape), axes, 0, 0, tiled=True
    )


CORES = [(0, 1), (1, 0)]
ROW_TILE = 256
UP_CHUNK = 640


def expert_kernel(keep, rows, own_up, other_up, own_down, other_down, *rest):
    out, up, down, up_sems, down_sem = rest[-5:]
    up_chunks = up.shape[0] // UP_CHUNK
    half_size = up.shape[1] // 2

    def up_copy(i, mine):
        part = pl.ds(i * UP_CHUNK, UP_CHUNK)
        source = own_up if mine else other_up
        return pltpu.make_async_copy(source.at[part], up.at[part], up_sems.at[i])

    def down_copy(mine):
        return pltpu.make_async_copy(own_down if mine else other_down, down, down_sem)

    def finish(joined, wait):
        gate = joined[:, :half_size]
        active = (gate / (1.0 + jnp.exp(-gate)) * joined[:, half_size:]).astype(jnp.bfloat16)
        if wait:
            down_copy(True).wait()
        out[...] = jnp.dot(active, down[...], preferred_element_type=jnp.float32).astype(jnp.bfloat16)

    @pl.when(pl.program_id(0) == 0)
    def _():
        @pl.when(keep[0] == 1)
        def _():
            for i in range(up_chunks):
                up_copy(i, True).start()
            down_copy(True).start()

        @pl.when(keep[0] == 0)
        def _():
            for i in range(up_chunks):
                up_copy(i, False).start()
            down_copy(False).start()

        joined = jnp.zeros((rows.shape[0], up.shape[1]), jnp.float32)
        for i in range(up_chunks):
            up_copy(i, True).wait()
            part = slice(i * UP_CHUNK, (i + 1) * UP_CHUNK)
            joined = joined + jnp.dot(
                rows[:, part], up[part, :], preferred_element_type=jnp.float32
            )
        finish(joined, True)

    @pl.when(pl.program_id(0) != 0)
    def _():
        finish(jnp.dot(rows[...], up[...], preferred_element_type=jnp.float32), False)


def expert_half(keep, rows, weights, first, tiles, filled=None):
    own_up, _, own_down, _ = weights
    anywhere = pl.BlockSpec(memory_space=pl.ANY)
    tile = pl.BlockSpec((ROW_TILE, rows.shape[1]), lambda i, keep: (first + i, 0))
    extra = [] if filled is None else [filled]
    return pl.pallas_call(
        expert_kernel,
        out_shape=jax.ShapeDtypeStruct(rows.shape, jnp.bfloat16),
        grid_spec=pltpu.PrefetchScalarGridSpec(
            num_scalar_prefetch=1,
            grid=(tiles,),
            in_specs=[tile] + [anywhere] * (4 + len(extra)),
            out_specs=tile,
            scratch_shapes=[
                pltpu.VMEM(own_up.shape, jnp.bfloat16),
                pltpu.VMEM(own_down.shape, jnp.bfloat16),
                pltpu.SemaphoreType.DMA((own_up.shape[0] // UP_CHUNK,)),
                pltpu.SemaphoreType.DMA,
            ],
        ),
        input_output_aliases={} if filled is None else {6: 0},
        compiler_params=pltpu.CompilerParams(
            dimension_semantics=("arbitrary",), vmem_limit_bytes=50 << 20
        ),
        cost_estimate=pl.CostEstimate(
            flops=2 * tiles * ROW_TILE * (own_up.size + own_down.size),
            transcendentals=tiles * ROW_TILE * own_down.shape[0],
            bytes_accessed=2 * (own_up.size + own_down.size)
            + 4 * tiles * ROW_TILE * rows.shape[1],
        ),
    )(keep, rows, *weights, *extra)


def per_device(
    hidden_in,
    placing,
    prompt_start,
    attn_gain,
    w_qkv,
    w_out,
    moe_gain,
    routes,
    route_weight,
    w_gate_up,
    w_down,
):
    row_count, model_width = hidden_in.shape
    query_width = QH * HD
    kv_width = KVH * HD
    my_index = lax.axis_index(CACHE)
    group_rows = placing.shape[0]
    cache_size = group_rows // row_count
    deal_rows = row_count // cache_size
    group_base = lax.axis_index(DP) * group_rows

    half_out = w_out.shape[1] // 2
    joint = jnp.concatenate(
        [w_qkv, jnp.concatenate([w_out[:, :half_out], w_out[:, half_out:]], axis=0)], axis=1
    )
    joint = spread(joint, CACHE, cache_size)
    qkv_rows = joint[:, :, : w_qkv.shape[1]].reshape(-1, w_qkv.shape[1])
    halves = joint[:, :, w_qkv.shape[1] :].reshape(cache_size, 2, w_out.shape[0], half_out)
    out_rows = jnp.concatenate([halves[:, 0], halves[:, 1]], axis=2).reshape(-1, w_out.shape[1])

    pairs = swap_pairs()
    sent_up, qkv_rows, out_rows = lax.optimization_barrier((w_gate_up[0], qkv_rows, out_rows))
    other_up = lax.ppermute(sent_up, ALL, pairs)
    keep = lax.axis_index("x") % 2 == lax.axis_index("core")

    full_qkv = lax.all_gather(qkv_rows, DP, axis=0, tiled=True)
    out_own = spread(out_rows, ("yh", "z"), 8).reshape(-1, w_out.shape[1])
    out_other = lax.ppermute(out_own, "core", CORES)
    full_qkv, other_up, out_own = lax.optimization_barrier((full_qkv, other_up, out_own))

    my_place = lax.dynamic_slice_in_dim(placing, my_index * row_count, row_count)
    position = my_place - prompt_start

    bits = routes
    chip_of = (
        (bits & 0b111000)
        | ((bits & 0b000011) << 1)
        | ((bits & 0b000100) >> 2)
    )
    named = chip_of[:, :, None] == jnp.arange(CHIP_COUNT, dtype=jnp.int32)[None, None, :]
    member = jnp.any(named, axis=1)
    weight_of = jnp.sum(jnp.where(named, route_weight[:, :, None], 0.0), axis=1)
    row_ids = jnp.arange(row_count, dtype=jnp.int32)
    before = (row_ids[:, None] > row_ids[None, :]).astype(jnp.bfloat16)
    rank = jnp.dot(before, member.astype(jnp.bfloat16), preferred_element_type=jnp.float32)
    rank = jnp.where(member, rank.astype(jnp.int32), -1).T
    chosen = rank[:, None, :] == jnp.arange(MOST, dtype=jnp.int32)[None, :, None]
    chosen = chosen.reshape(CHIP_COUNT * MOST, row_count)
    pick = chosen.astype(jnp.bfloat16)
    weighted = jnp.where(
        chosen.reshape(CHIP_COUNT, MOST, row_count), weight_of.T[:, None, :], 0.0
    ).reshape(CHIP_COUNT * MOST, row_count)
    weighted_hi = lax.reduce_precision(weighted, 8, 7)
    weighted_lo = (weighted - weighted_hi).astype(jnp.bfloat16)
    blend = jnp.concatenate([weighted_hi.astype(jnp.bfloat16), weighted_lo], axis=1)

    normed = rms_scaled(hidden_in, attn_gain)
    core = lax.axis_index("core")
    projected = jnp.dot(normed, full_qkv, preferred_element_type=jnp.float32)
    half_size = HD // 2
    inverse = rope_base ** (-(jnp.arange(half_size, dtype=jnp.float32) * 2.0 / HD))
    angles = position.astype(jnp.float32)[:, None] * inverse[None, :]
    cosine = jnp.cos(angles)
    sine_part = jnp.sin(angles)
    keys_here = [
        rotated(projected[:, query_width + k * HD : query_width + (k + 1) * HD], cosine, sine_part)
        for k in range(KVH)
    ]
    values_here = projected[:, query_width + kv_width :].astype(jnp.bfloat16)
    kv_here = jnp.concatenate(keys_here + [values_here], axis=1)
    kv_group = spread(kv_here, CACHE, cache_size).reshape(group_rows, 2 * kv_width)
    kv_group, sent_down = lax.optimization_barrier((kv_group, w_down[0]))
    other_down = lax.ppermute(sent_down, ALL, pairs)
    queries = jnp.stack(
        [rotated(projected[:, h * HD : (h + 1) * HD], cosine, sine_part) for h in range(QH)]
    )
    allowed = (placing[None, :] >= prompt_start[:, None]) & (placing[None, :] <= my_place[:, None])
    contexts = []
    share = QH // KVH
    for k in range(KVH):
        key_head = kv_group[:, k * HD : (k + 1) * HD]
        value_head = kv_group[:, kv_width + k * HD : kv_width + (k + 1) * HD]
        scores = jnp.einsum(
            "htd,rd->htr",
            queries[k * share : (k + 1) * share],
            key_head,
            preferred_element_type=jnp.float32,
        ) * (HD ** (-0.5))
        scores = jnp.where(allowed[None], scores, masked_score)
        highest = jnp.max(scores, axis=-1, keepdims=True)
        weights = jnp.where(allowed[None], jnp.exp(scores - highest), 0.0)
        denominator = jnp.sum(weights, axis=-1, keepdims=True)
        numerator = jnp.einsum(
            "htr,rd->htd",
            weights.astype(jnp.bfloat16),
            value_head,
            preferred_element_type=jnp.float32,
        )
        contexts.append((numerator / denominator).astype(jnp.bfloat16))
    context = jnp.concatenate(contexts, axis=0)
    context = jnp.concatenate([context[h] for h in range(QH)], axis=1)
    order = jnp.arange(query_width, dtype=jnp.int32)
    span = query_width // 2
    piece = w_out.shape[0] * cache_size
    at_core = jnp.where(order < span, core, 1 - core)
    inner = order % span
    source = (inner // piece * 2 + at_core) * piece + inner % piece
    take = (order[:, None] == source[None, :]).astype(jnp.bfloat16)
    take = lax.optimization_barrier(take)
    context = jnp.dot(context, take, preferred_element_type=jnp.float32).astype(jnp.bfloat16)
    attn_out = jnp.dot(context[:, :span], out_own, preferred_element_type=jnp.float32)
    attn_out = attn_out + jnp.dot(context[:, span:], out_other, preferred_element_type=jnp.float32)
    attended = (hidden_in.astype(jnp.float32) + attn_out).astype(jnp.bfloat16)
    moe_in = rms_scaled(attended, moe_gain)

    outgoing = jnp.dot(pick, moe_in, preferred_element_type=jnp.float32).astype(jnp.bfloat16)
    outgoing, other_down = lax.optimization_barrier((outgoing, other_down))
    mine = lax.all_to_all(
        outgoing.reshape(CHIP_COUNT, MOST, model_width), CHIPS, 0, 0, tiled=True
    ).reshape(CHIP_COUNT * MOST, model_width)
    mates = lax.ppermute(mine, "core", CORES)
    weights = (w_gate_up[0], other_up, w_down[0], other_down)
    kept = keep.astype(jnp.int32).reshape(1)
    tiles = mine.shape[0] // ROW_TILE
    own_part = expert_half(kept, mine, weights, 0, tiles // 2)
    mates, own_part = lax.optimization_barrier((mates, own_part))
    for_mate = expert_half(kept, mates, weights, 0, tiles)
    from_mate = lax.ppermute(for_mate, "core", CORES)
    own_part = expert_half(kept, mine, weights, tiles // 2, tiles // 2, own_part)
    expert_out = (own_part.astype(jnp.float32) + from_mate.astype(jnp.float32)).astype(jnp.bfloat16)
    returned = lax.all_to_all(
        expert_out.reshape(CHIP_COUNT, MOST, model_width), CHIPS, 0, 0, tiled=True
    ).reshape(CHIP_COUNT * MOST, model_width)
    blended = lax.dot_general(
        blend, returned, (((0,), (0,)), ((), ())), preferred_element_type=jnp.float32
    )
    mixture = blended[:row_count] + blended[row_count:]
    finished = (attended.astype(jnp.float32) + mixture).astype(jnp.bfloat16)

    home_rows = lax.all_to_all(
        finished.reshape(cache_size, deal_rows, model_width), CACHE, 0, 0, tiled=True
    ).reshape(row_count, model_width)
    my_base = group_base + my_index * row_count
    sender_place = lax.dynamic_slice_in_dim(
        placing.reshape(cache_size, row_count), my_index * deal_rows, deal_rows, axis=1
    ).reshape(-1)
    to_row = (sender_place[None, :] - my_base == row_ids[:, None]).astype(jnp.bfloat16)
    mixed = jnp.dot(to_row, home_rows, preferred_element_type=jnp.float32).astype(jnp.bfloat16)
    from_group = (placing[None, :] - my_base == row_ids[:, None]).astype(jnp.bfloat16)
    cached = jnp.dot(from_group, kv_group, preferred_element_type=jnp.float32).astype(jnp.bfloat16)
    return (mixed, cached[:, :kv_width], cached[:, kv_width:])


def solution(mesh):
    fine = Mesh(np.asarray(mesh.devices).reshape(tuple(SIZES[a] for a in ALL)), ALL)
    in_specs = (
        P(ALL, None),
        P(DP),
        P(ALL),
        P(),
        P(ALL, None),
        P(ALL, None),
        P(),
        P(ALL, None),
        P(ALL, None),
        P(ALL, None, None),
        P(ALL, None, None),
    )
    out_specs = (P(ALL, None), P(ALL, None), P(ALL, None))
    return jax.shard_map(
        per_device, mesh=fine, in_specs=in_specs, out_specs=out_specs, check_vma=False
    )
```

profile of v0, /device:TPU:1, one launch (start us, length us, event | category | flops | bytes accessed | tf_op | source)
XLA Modules:
  0.0 446.9 jit_solution(16786242520701570411)
XLA Ops:
  9.1 22.0 %all_to_all.30 = bf16[8,20,3072]{2,1,0:T(8,128)(2,1)S(1)} all-to-all(bf16[8,20,3072]{2,1,0:T(8,128)(2,1)S(1)} %broadcast_in_dim.71), channel_id=1, replica_groups=mesh['yh'=2,'z'=4,'core'=2,'yl'=2,'x'=4] {'yl','x'}, dimensions={0} | all-to-all | bytes 1966080 | tf_op jit(solution)/shard_map/all_to_all | solution.py:61
  32.6 4.2 collective-permute-start
  38.8 7.4 %all-to-all-start.1 = ((bf16[8,80,2560]{2,1,0:T(8,128)(2,1)}), bf16[8,80,2560]{2,1,0:T(8,128)(2,1)S(1)}, u32[]{:S(2)}, u32[]{:S(2)}) async-start(bf16[8,80,2560]{2,1,0:T(8,128)(2,1)} %broadcast_in_dim.72), calls=%async_computation.1 | async-start | bytes 6553600 | tf_op jit(solution)/shard_map/all_to_all | solution.py:61
  46.3 3.1 fusion.2
  52.1 40.8 %all-to-all-done.1 = bf16[8,80,2560]{2,1,0:T(8,128)(2,1)S(1)} async-done(((bf16[8,80,2560]{2,1,0:T(8,128)(2,1)}), bf16[8,80,2560]{2,1,0:T(8,128)(2,1)S(1)}, u32[]{:S(2)}, u32[]{:S(2)}) %all-to-all-start.1) | async-done | bytes 3276832 | tf_op jit(solution)/shard_map/all_to_all | solution.py:61
  93.7 29.1 %collective-permute-done.other_up = bf16[2560,1536]{1,0:T(8,128)(2,1)} collective-permute-done((bf16[2560,1536]{1,0:T(8,128)(2,1)}, bf16[2560,1536]{1,0:T(8,128)(2,1)}, u32[]{:S(2)}, u32[]{:S(2)}) %collective-permute-start) | collective-permute-done | bytes 7864352 | tf_op jit(solution)/shard_map/ppermute | solution.py:185
  122.9 21.7 %all-gather.2.cloned.1.call-done = bf16[2560,1792]{1,0:T(8,128)(2,1)} async-done(((bf16[160,1792]{1,0:T(8,128)(2,1)}), bf16[2560,1792]{1,0:T(8,128)(2,1)}) %all-gather.2.cloned.1.call-update) | async-done | bytes 9175056 | tf_op jit(solution)/shard_map/all_gather | solution.py:188
  144.5 5.2 %fusion.36 = f32[128,1792]{1,0:T(8,128)S(1)} fusion(bf16[2560,1792]{1,0:T(8,128)(2,1)} %all-gather.2.cloned.1.call-done, bf16[128,2560]{1,0:T(8,128)(2,1)} %param.11, f32[2560]{0:T(1024)S(1)} %copy-done.8, f32[128]{0:T(128)S(1)} %add_rsqrt_fusion.1), kind=kOutput, calls=%fused_computation.47 | convolution fusion | flops 1175715840 | bytes 10758656 | tf_op jit(solution)/shard_map/dot_general | solution.py:221
  154.6 4.4 all-to-all-start.2
  170.6 4.3 all-to-all-done.2
  174.9 3.3 collective-permute-start.2
  180.6 3.2 fusion.32
  192.9 3.2 fusion.29
  210.8 11.5 %collective-permute-done.2.other_down = bf16[768,2560]{1,0:T(8,128)(2,1)} collective-permute-done((bf16[768,2560]{1,0:T(8,128)(2,1)}, bf16[768,2560]{1,0:T(8,128)(2,1)}, u32[]{:S(2)}, u32[]{:S(2)}) %collective-permute-start.2) | collective-permute-done | bytes 3932192 | tf_op jit(solution)/shard_map/ppermute | solution.py:235
  222.3 68.3 %all_to_all.31 = bf16[64,16,2560]{2,1,0:T(8,128)(2,1)} all-to-all(bf16[64,16,2560]{2,1,0:T(8,128)(2,1)S(1)} %bitcast.164), channel_id=1, replica_groups=mesh['yh'=2,'z'=4,'core'=2,'yl'=2,'x'=4] {'yh','z','yl','x'}, dimensions={0} | all-to-all | bytes 10485760 | tf_op jit(solution)/shard_map/all_to_all | solution.py:280
  294.3 11.8 %shard_map.130.rest_0_ = bf16[1024,2560]{1,0:T(8,128)(2,1)} custom-call(s32[1]{0:T(128)} %bitcast.44.keep, bf16[1024,2560]{1,0:T(8,128)(2,1)} %bitcast.46.rows, bf16[2560,1536]{1,0:T(8,128)(2,1)} %bitcast.166, bf16[2560,1536]{1,0:T(8,128)(2,1)} %collective-permute-done.other_up, bf16[768,2560]{1,0:T(8,128)(2,1)S(1)} %bitcast.161, ...), custom_call_target="tpu_custom_call" | custom-call | flops 6039797760 | bytes 17039360 | tf_op jit(solution)/shard_map/pallas_call | solution.py:124
  306.1 18.3 %shard_map.132 = bf16[1024,2560]{1,0:T(8,128)(2,1)} custom-call(s32[1]{0:T(128)} %bitcast.44.keep, bf16[1024,2560]{1,0:T(8,128)(2,1)} %collective-permute-done.3.rows, bf16[2560,1536]{1,0:T(8,128)(2,1)} %bitcast.167, bf16[2560,1536]{1,0:T(8,128)(2,1)} %collective-permute-done.other_up, bf16[768,2560]{1,0:T(8,128)(2,1)S(1)} %bitcast.162, ...), custom_call_target="tpu_custom_call" | custom-call | flops 12079595520 | bytes 22282240 | tf_op jit(solution)/shard_map/pallas_call | solution.py:124
  324.8 11.8 %shard_map.131 = bf16[1024,2560]{1,0:T(8,128)(2,1)} custom-call(s32[1]{0:T(128)} %bitcast.44.keep, bf16[1024,2560]{1,0:T(8,128)(2,1)} %bitcast.46.rows, bf16[2560,1536]{1,0:T(8,128)(2,1)} %bitcast.168, bf16[2560,1536]{1,0:T(8,128)(2,1)} %collective-permute-done.other_up, bf16[768,2560]{1,0:T(8,128)(2,1)S(1)} %bitcast.163, ...), custom_call_target="tpu_custom_call", output_to_operand_aliasing={{}: (6, {})} | custom-call | flops 6039797760 | bytes 17039360 | tf_op jit(solution)/shard_map/pallas_call | solution.py:124
  336.6 6.3 %add_convert_fusion = bf16[1024,2560]{1,0:T(8,128)(2,1)} fusion(bf16[1024,2560]{1,0:T(8,128)(2,1)S(1)} %collective-permute-done.4, bf16[1024,2560]{1,0:T(8,128)(2,1)} %shard_map.131), kind=kLoop, calls=%fused_computation.2 | loop fusion | flops 10485760 | bytes 15728640 | tf_op jit(solution)/shard_map/convert_element_type | solution.py:292
  342.9 5.8 %all-to-all-start.4 = ((bf16[64,16,2560]{2,1,0:T(8,128)(2,1)}), bf16[64,16,2560]{2,1,0:T(8,128)(2,1)}, u32[]{:S(2)}, u32[]{:S(2)}) async-start(bf16[64,16,2560]{2,1,0:T(8,128)(2,1)} %bitcast.169), calls=%async_computation.4 | async-start | bytes 10485760 | tf_op jit(solution)/shard_map/all_to_all | solution.py:293
  349.0 69.4 %all-to-all-done.4 = bf16[64,16,2560]{2,1,0:T(8,128)(2,1)} async-done(((bf16[64,16,2560]{2,1,0:T(8,128)(2,1)}), bf16[64,16,2560]{2,1,0:T(8,128)(2,1)}, u32[]{:S(2)}, u32[]{:S(2)}) %all-to-all-start.4) | async-done | bytes 5242912 | tf_op jit(solution)/shard_map/all_to_all | solution.py:293
  418.4 4.1 fusion.43
  423.6 4.0 all-to-all-start.5
  429.9 9.0 %all-to-all-done.5 = bf16[8,16,2560]{2,1,0:T(8,128)(2,1)S(1)} async-done(((bf16[8,16,2560]{2,1,0:T(8,128)(2,1)}), bf16[8,16,2560]{2,1,0:T(8,128)(2,1)S(1)}, u32[]{:S(2)}, u32[]{:S(2)}) %all-to-all-start.5) | async-done | bytes 655392 | tf_op jit(solution)/shard_map/all_to_all | solution.py:302
  (105 shorter events, 60.4 us)
Async XLA Ops:
  7.2 137.4 %all-gather.2.cloned.1.call-start = ((), (), s32[]{:S(2)}) async-start(), calls=%async_computation.6 | async-start | bytes 9748480 | tf_op jit(solution)/shard_map/all_gather | solution.py:188
  32.6 90.3 %collective-permute-start = (bf16[2560,1536]{1,0:T(8,128)(2,1)}, bf16[2560,1536]{1,0:T(8,128)(2,1)}, u32[]{:S(2)}, u32[]{:S(2)}) collective-permute-start(bf16[2560,1536]{1,0:T(8,128)(2,1)} %bitcast.165), channel_id=1, source_target_pairs={{8,1},{1,8},{10,3},{3,10},{12,5},{5,12},{14,7},{7,14},{24,17},{17,... | collective-permute-start | bytes 23592968 | tf_op jit(solution)/shard_map/ppermute | solution.py:185
  38.8 54.0 %all-to-all-start.1 = ((bf16[8,80,2560]{2,1,0:T(8,128)(2,1)}), bf16[8,80,2560]{2,1,0:T(8,128)(2,1)S(1)}, u32[]{:S(2)}, u32[]{:S(2)}) async-start(bf16[8,80,2560]{2,1,0:T(8,128)(2,1)} %broadcast_in_dim.72), calls=%async_computation.1 | async-start | bytes 6553600 | tf_op jit(solution)/shard_map/all_to_all | solution.py:61
  46.2 3.2 copy-start.13
  46.2 5.0 %copy-start.9 = (s32[1024]{0:T(1024)S(1)}, s32[1024]{0:T(1024)}, u32[]{:S(2)}) copy-start(s32[1024]{0:T(1024)} %param.12) | copy-start | bytes 12292
  46.2 5.0 %copy-start.14 = (s32[128]{0:T(128)S(1)}, s32[128]{0:T(128)}, u32[]{:S(2)}) copy-start(s32[128]{0:T(128)} %param.13) | copy-start | bytes 1540
  46.2 98.4 %copy-start.8 = (f32[2560]{0:T(1024)S(1)}, f32[2560]{0:T(1024)}, u32[]{:S(2)}) copy-start(f32[2560]{0:T(1024)} %param.14) | copy-start | bytes 30724
  49.6 1.7 copy-start.6
  49.8 101.7 %copy-start.11 = (f32[64]{0:T(128)}, f32[64]{0:T(128)S(1)}, u32[]{:S(2)}) copy-start(f32[64]{0:T(128)S(1)} %negate_power_fusion) | copy-start | bytes 772
  92.8 112.8 %collective-permute-start.1 = (bf16[640,2560]{1,0:T(8,128)(2,1)S(1)}, bf16[640,2560]{1,0:T(8,128)(2,1)}, u32[]{:S(2)}, u32[]{:S(2)}) collective-permute-start(bf16[640,2560]{1,0:T(8,128)(2,1)S(1)} %bitcast.170), channel_id=1, source_target_pairs={{0,8},{8,0},{1,9},{9,1},{2,10},{10,2},{3,11},{11,3},{4,12},{12,4},... | collective-permute-start | bytes 9830408 | tf_op jit(solution)/shard_map/ppermute | solution.py:190
  149.8 1.7 copy-start.4
  154.6 23.6 %copy-start.5 = (pred[128,1024]{1,0:T(8,128)(4,1)S(1)}, pred[128,1024]{1,0:T(8,128)(4,1)}, u32[]{:S(2)}) copy-start(pred[128,1024]{1,0:T(8,128)(4,1)} %compare_and_fusion) | copy-start | bytes 393220
  154.6 20.3 %all-to-all-start.2 = ((bf16[8,128,512]{2,1,0:T(8,128)(2,1)}), bf16[8,128,512]{2,1,0:T(8,128)(2,1)}, u32[]{:S(2)}, u32[]{:S(2)}) async-start(bf16[8,128,512]{2,1,0:T(8,128)(2,1)} %broadcast_in_dim.116), calls=%async_computation.2 | async-start | bytes 2097152 | tf_op jit(solution)/shard_map/all_to_all | solution.py:61
  174.9 47.3 %collective-permute-start.2 = (bf16[768,2560]{1,0:T(8,128)(2,1)}, bf16[768,2560]{1,0:T(8,128)(2,1)}, u32[]{:S(2)}, u32[]{:S(2)}) collective-permute-start(bf16[768,2560]{1,0:T(8,128)(2,1)} %bitcast.160), channel_id=1, source_target_pairs={{8,1},{1,8},{10,3},{3,10},{12,5},{5,12},{14,7},{7,14},{24,17},{17,... | collective-permute-start | bytes 11796488 | tf_op jit(solution)/shard_map/ppermute | solution.py:235
  205.6 2.7 copy-start.3
  209.1 1.6 copy-start.1
  290.5 15.6 %collective-permute-start.3 = (bf16[1024,2560]{1,0:T(8,128)(2,1)}, bf16[1024,2560]{1,0:T(8,128)(2,1)}, u32[]{:S(2)}, u32[]{:S(2)}) collective-permute-start(bf16[1024,2560]{1,0:T(8,128)(2,1)} %bitcast.46.rows), channel_id=1, source_target_pairs={{0,8},{8,0},{1,9},{9,1},{2,10},{10,2},{3,11},{11,3},{4,12},{12,4},... | collective-permute-start | bytes 15728648 | tf_op jit(solution)/shard_map/ppermute | solution.py:283
  292.2 2.1 copy-start
  324.4 12.2 %collective-permute-start.4 = (bf16[1024,2560]{1,0:T(8,128)(2,1)}, bf16[1024,2560]{1,0:T(8,128)(2,1)S(1)}, u32[]{:S(2)}, u32[]{:S(2)}) collective-permute-start(bf16[1024,2560]{1,0:T(8,128)(2,1)} %shard_map.132), channel_id=1, source_target_pairs={{0,8},{8,0},{1,9},{9,1},{2,10},{10,2},{3,11},{11,3},{4,12},{12,4},... | collective-permute-start | bytes 15728648 | tf_op jit(solution)/shard_map/ppermute | solution.py:290
  342.9 5.8 %copy-start.12 = (f32[128,6]{0,1:T(8,128)S(1)}, f32[128,6]{0,1:T(8,128)}, u32[]{:S(2)}) copy-start(f32[128,6]{0,1:T(8,128)} %param.19) | copy-start | bytes 9220
  342.9 5.9 %copy-start.7 = (s32[64,128]{1,0:T(8,128)S(1)}, s32[64,128]{1,0:T(8,128)}, u32[]{:S(2)}) copy-start(s32[64,128]{1,0:T(8,128)} %copy-done.6) | copy-start | bytes 98308
  342.9 75.5 %all-to-all-start.4 = ((bf16[64,16,2560]{2,1,0:T(8,128)(2,1)}), bf16[64,16,2560]{2,1,0:T(8,128)(2,1)}, u32[]{:S(2)}, u32[]{:S(2)}) async-start(bf16[64,16,2560]{2,1,0:T(8,128)(2,1)} %bitcast.169), calls=%async_computation.4 | async-start | bytes 10485760 | tf_op jit(solution)/shard_map/all_to_all | solution.py:293
  418.4 4.1 copy-start.2
  423.6 15.4 %all-to-all-start.5 = ((bf16[8,16,2560]{2,1,0:T(8,128)(2,1)}), bf16[8,16,2560]{2,1,0:T(8,128)(2,1)S(1)}, u32[]{:S(2)}, u32[]{:S(2)}) async-start(bf16[8,16,2560]{2,1,0:T(8,128)(2,1)} %bitcast.49), calls=%async_computation.5 | async-start | bytes 1310720 | tf_op jit(solution)/shard_map/all_to_all | solution.py:302
  (1 other events, 0.9 us)
Sparse Core Ops, SparseCore 0:
  32.7 111.7 all-gather.1
where the time goes:
time: 450 us; the launch traced here: 447 us
  waiting for transfers between devices  186 us (41%)
  blocking collectives  90.3 us (20%)
  Pallas kernels  41.9 us (9%)
  starting transfers between devices  32 us (7%)
  matrix products  30.9 us (7%)
  other arithmetic  27.8 us (6%)
  local copies, waits for them, and re-layouts  23.8 us (5%)
  between operations  14.5 us (3%)
    all_to_all x1, waiting for transfers between devices, per_device(): lax.all_to_all(expert_out.reshape(CHIP_COUNT, MOST, model_width), CHIPS,...  69.4 us
    all_to_all x1, blocking collectives, per_device(): lax.all_to_all(outgoing.reshape(CHIP_COUNT, MOST, model_width), CHIPS, 0,...  68.3 us
    all_to_all x2, waiting for transfers between devices, spread(): lax.all_to_all(jnp.broadcast_to(shard[None], (count,) + shard.shape), axe...  45.1 us
    pallas_call x3, Pallas kernels, expert_half(): pl.pallas_call(expert_kernel, out_shape=jax.ShapeDtypeStruct(rows.shape,...  41.9 us
    ppermute x1, waiting for transfers between devices, per_device(): other_up = lax.ppermute(sent_up, ALL, pairs)  29.1 us
    all_to_all x1, blocking collectives, spread(): lax.all_to_all(jnp.broadcast_to(shard[None], (count,) + shard.shape), axe...  22 us
    all_gather x1, waiting for transfers between devices, per_device(): full_qkv = lax.all_gather(qkv_rows, DP, axis=0, tiled=True)  21.7 us
    unnamed x40, local copies, waits for them, and re-layouts  14.6 us
  transfers between devices with their start and end apart: 10, of which 7 were waited for; matrix products, arithmetic and copies ran while one was open for 14% of the time, Pallas kernels for 5%

commit v1 on v0

--- a/solution.py
+++ b/solution.py
@@ -47,14 +47,80 @@
     return (widened * factor * gain_vector).astype(jnp.bfloat16)
 
 
-def rotated(grouped, cosine, sine_part):
-    half_size = HD // 2
-    first_half = grouped[..., :half_size]
-    second = grouped[..., half_size:]
-    return jnp.concatenate(
-        [first_half * cosine - second * sine_part, second * cosine + first_half * sine_part],
-        axis=-1,
-    ).astype(jnp.bfloat16)
+def turned(head, cosines, sines):
+    return (head * cosines + pltpu.roll(head, HD // 2, 1) * sines).astype(jnp.bfloat16)
+
+
+def keys_values_kernel(normed, w_block, cosines, sines, out):
+    block = jnp.dot(normed[...], w_block[...], preferred_element_type=jnp.float32)
+
+    def write(columns, part):
+        for copy in range(out.shape[0]):
+            out[copy, :, columns] = part
+
+    @pl.when(pl.program_id(0) == 0)
+    def _():
+        for k in range(KVH):
+            columns = slice(k * HD, (k + 1) * HD)
+            write(columns, turned(block[:, columns], cosines[...], sines[...]))
+
+    @pl.when(pl.program_id(0) == 1)
+    def _():
+        write(slice(0, KVH * HD), block.astype(jnp.bfloat16))
+
+
+def keys_values(normed, w_qkv, cosines, sines, copies):
+    row_count, model_width = normed.shape
+    width = KVH * HD
+    whole = lambda i: (0, 0)
+    return pl.pallas_call(
+        keys_values_kernel,
+        out_shape=jax.ShapeDtypeStruct((copies, row_count, 2 * width), jnp.bfloat16),
+        grid=(2,),
+        in_specs=[
+            pl.BlockSpec((row_count, model_width), whole),
+            pl.BlockSpec((model_width, width), lambda i: (0, QH * HD // width + i)),
+            pl.BlockSpec((row_count, HD), whole),
+            pl.BlockSpec((row_count, HD), whole),
+        ],
+        out_specs=pl.BlockSpec((copies, row_count, width), lambda i: (0, 0, i)),
+        compiler_params=pltpu.CompilerParams(
+            dimension_semantics=("arbitrary",), vmem_limit_bytes=32 << 20
+        ),
+    )(normed, w_qkv, cosines, sines)
+
+
+def attention_kernel(projected, cosines, sines, kv_group, placing, start, place, out):
+    allowed = (placing[...] >= start[...]) & (placing[...] <= place[...])
+    share = QH // KVH
+    for h in range(QH):
+        columns = slice(h * HD, (h + 1) * HD)
+        k = h // share
+        query = turned(projected[:, columns], cosines[...], sines[...])
+        scores = lax.dot_general(
+            query,
+            kv_group[:, k * HD : (k + 1) * HD],
+            (((1,), (1,)), ((), ())),
+            preferred_element_type=jnp.float32,
+        ) * (HD ** (-0.5))
+        scores = jnp.where(allowed, scores, masked_score)
+        highest = jnp.max(scores, axis=1, keepdims=True)
+        weights = jnp.where(allowed, jnp.exp(scores - highest), 0.0)
+        denominator = jnp.sum(weights, axis=1, keepdims=True)
+        numerator = jnp.dot(
+            weights.astype(jnp.bfloat16),
+            kv_group[:, (KVH + k) * HD : (KVH + k + 1) * HD],
+            preferred_element_type=jnp.float32,
+        )
+        out[:, columns] = (numerator / denominator).astype(jnp.bfloat16)
+
+
+def attention(projected, *operands):
+    return pl.pallas_call(
+        attention_kernel,
+        out_shape=jax.ShapeDtypeStruct(projected.shape, jnp.bfloat16),
+        compiler_params=pltpu.CompilerParams(vmem_limit_bytes=32 << 20),
+    )(projected, *operands)
 
 
 def spread(shard, axes, count):
@@ -186,9 +252,8 @@
     keep = lax.axis_index("x") % 2 == lax.axis_index("core")
 
     full_qkv = lax.all_gather(qkv_rows, DP, axis=0, tiled=True)
-    out_own = spread(out_rows, ("yh", "z"), 8).reshape(-1, w_out.shape[1])
-    out_other = lax.ppermute(out_own, "core", CORES)
-    full_qkv, other_up, out_own = lax.optimization_barrier((full_qkv, other_up, out_own))
+    full_out = lax.all_gather(out_rows, DP, axis=0, tiled=True)
+    full_qkv, other_up = lax.optimization_barrier((full_qkv, other_up))
 
     my_place = lax.dynamic_slice_in_dim(placing, my_index * row_count, row_count)
     position = my_place - prompt_start
@@ -217,61 +282,22 @@
     blend = jnp.concatenate([weighted_hi.astype(jnp.bfloat16), weighted_lo], axis=1)
 
     normed = rms_scaled(hidden_in, attn_gain)
-    core = lax.axis_index("core")
-    projected = jnp.dot(normed, full_qkv, preferred_element_type=jnp.float32)
     half_size = HD // 2
     inverse = rope_base ** (-(jnp.arange(half_size, dtype=jnp.float32) * 2.0 / HD))
     angles = position.astype(jnp.float32)[:, None] * inverse[None, :]
     cosine = jnp.cos(angles)
     sine_part = jnp.sin(angles)
-    keys_here = [
-        rotated(projected[:, query_width + k * HD : query_width + (k + 1) * HD], cosine, sine_part)
-        for k in range(KVH)
-    ]
-    values_here = projected[:, query_width + kv_width :].astype(jnp.bfloat16)
-    kv_here = jnp.concatenate(keys_here + [values_here], axis=1)
-    kv_group = spread(kv_here, CACHE, cache_size).reshape(group_rows, 2 * kv_width)
-    kv_group, sent_down = lax.optimization_barrier((kv_group, w_down[0]))
+    cosines = jnp.concatenate([cosine, cosine], axis=1)
+    sines = jnp.concatenate([-sine_part, sine_part], axis=1)
+    kv_copies = keys_values(normed, full_qkv, cosines, sines, cache_size)
+    kv_group = lax.all_to_all(kv_copies, CACHE, 0, 0, tiled=True).reshape(group_rows, 2 * kv_width)
+    projected = jnp.dot(normed, full_qkv[:, :query_width], preferred_element_type=jnp.float32)
+    kv_group, projected, sent_down = lax.optimization_barrier((kv_group, projected, w_down[0]))
     other_down = lax.ppermute(sent_down, ALL, pairs)
-    queries = jnp.stack(
-        [rotated(projected[:, h * HD : (h + 1) * HD], cosine, sine_part) for h in range(QH)]
-    )
-    allowed = (placing[None, :] >= prompt_start[:, None]) & (placing[None, :] <= my_place[:, None])
-    contexts = []
-    share = QH // KVH
-    for k in range(KVH):
-        key_head = kv_group[:, k * HD : (k + 1) * HD]
-        value_head = kv_group[:, kv_width + k * HD : kv_width + (k + 1) * HD]
-        scores = jnp.einsum(
-            "htd,rd->htr",
-            queries[k * share : (k + 1) * share],
-            key_head,
-            preferred_element_type=jnp.float32,
-        ) * (HD ** (-0.5))
-        scores = jnp.where(allowed[None], scores, masked_score)
-        highest = jnp.max(scores, axis=-1, keepdims=True)
-        weights = jnp.where(allowed[None], jnp.exp(scores - highest), 0.0)
-        denominator = jnp.sum(weights, axis=-1, keepdims=True)
-        numerator = jnp.einsum(
-            "htr,rd->htd",
-            weights.astype(jnp.bfloat16),
-            value_head,
-            preferred_element_type=jnp.float32,
-        )
-        contexts.append((numerator / denominator).astype(jnp.bfloat16))
-    context = jnp.concatenate(contexts, axis=0)
-    context = jnp.concatenate([context[h] for h in range(QH)], axis=1)
-    order = jnp.arange(query_width, dtype=jnp.int32)
-    span = query_width // 2
-    piece = w_out.shape[0] * cache_size
-    at_core = jnp.where(order < span, core, 1 - core)
-    inner = order % span
-    source = (inner // piece * 2 + at_core) * piece + inner % piece
-    take = (order[:, None] == source[None, :]).astype(jnp.bfloat16)
-    take = lax.optimization_barrier(take)
-    context = jnp.dot(context, take, preferred_element_type=jnp.float32).astype(jnp.bfloat16)
-    attn_out = jnp.dot(context[:, :span], out_own, preferred_element_type=jnp.float32)
-    attn_out = attn_out + jnp.dot(context[:, span:], out_other, preferred_element_type=jnp.float32)
+    context = attention(
+        projected, cosines, sines, kv_group, placing[None, :], prompt_start[:, None], my_place[:, None]
+    )
+    attn_out = jnp.dot(context, full_out, preferred_element_type=jnp.float32)
     attended = (hidden_in.astype(jnp.float32) + attn_out).astype(jnp.bfloat16)
     moe_in = rms_scaled(attended, moe_gain)
 

time: 450 us -> 432 us (0.960)
  waiting for transfers between devices: 186 us -> 208 us
  other arithmetic: 27.8 us -> 10.4 us
  matrix products: 30.9 us -> 15.3 us
  local copies, waits for them, and re-layouts: 23.8 us -> 9.1 us
  starting transfers between devices: 32 us -> 22.7 us
  blocking collectives: 90.3 us -> 99 us
  Pallas kernels: 41.9 us -> 47.9 us
    ppermute x1, waiting for transfers between devices: 29.1 us -> 84.8 us  [per_device(): other_up = lax.ppermute(sent_up, ALL, pairs)]
    all_to_all x2 -> x1, waiting for transfers between devices: 45.1 us -> 11.9 us  [per_device(): lax.all_to_all(kv_copies, CACHE, 0, 0, tiled=True)]
    all_gather x0 -> x1, waiting for transfers between devices: none -> 23.2 us  [per_device(): full_out = lax.all_gather(out_rows, DP, axis=0, tiled=True)]
    all_gather x1, waiting for transfers between devices: 21.7 us -> 0.01 us  [per_device(): full_qkv = lax.all_gather(qkv_rows, DP, axis=0, tiled=True)]
    dot_general x6 -> x2, matrix products: 17.7 us -> 7.91 us  [the longest x1 3.99 us: per_device(): attn_out = jnp.dot(context, full_out, preferred_element_type=jnp.float32)]
    unnamed x40 -> x23, local copies, waits for them, and re-layouts: 14.6 us -> 5.84 us
    all_to_all x1, blocking collectives: 68.3 us -> 77 us  [per_device(): lax.all_to_all(outgoing.reshape(CHIP_COUNT, MOST, model_width), CHIPS, 0,...]
    all_to_all x2 -> x1, starting transfers between devices: 11.7 us -> 3.56 us  [per_device(): lax.all_to_all(kv_copies, CACHE, 0, 0, tiled=True)]
  transfers between devices with their start and end apart: 10 -> 9, of which waited for: 7 -> 6; matrix products, arithmetic and copies ran while one was open for 14% -> 3% of each run, Pallas kernels for 5% -> 7%
where the time goes in v1:
time: 432 us; the launch traced here: 427 us
  waiting for transfers between devices  208 us (48%)
  blocking collectives  99 us (23%)
  Pallas kernels  47.9 us (11%)
  starting transfers between devices  22.7 us (5%)
  matrix products  15.3 us (4%)
  between operations  14.5 us (3%)
  other arithmetic  10.4 us (2%)
  local copies, waits for them, and re-layouts  9.1 us (2%)
    ppermute x1, waiting for transfers between devices, per_device(): other_up = lax.ppermute(sent_up, ALL, pairs)  84.8 us
    all_to_all x1, blocking collectives, per_device(): lax.all_to_all(outgoing.reshape(CHIP_COUNT, MOST, model_width), CHIPS, 0,...  77 us
    all_to_all x1, waiting for transfers between devices, per_device(): lax.all_to_all(expert_out.reshape(CHIP_COUNT, MOST, model_width), CHIPS,...  69.9 us
    pallas_call x3, Pallas kernels, expert_half(): pl.pallas_call(expert_kernel, out_shape=jax.ShapeDtypeStruct(rows.shape,...  41.9 us
    all_gather x1, waiting for transfers between devices, per_device(): full_out = lax.all_gather(out_rows, DP, axis=0, tiled=True)  23.2 us
    all_to_all x1, blocking collectives, spread(): lax.all_to_all(jnp.broadcast_to(shard[None], (count,) + shard.shape), axe...  22 us
    all_to_all x1, waiting for transfers between devices, per_device(): lax.all_to_all(kv_copies, CACHE, 0, 0, tiled=True)  11.9 us
    ppermute x1, waiting for transfers between devices, per_device(): other_down = lax.ppermute(sent_down, ALL, pairs)  10.3 us
  transfers between devices with their start and end apart: 9, of which 6 were waited for; matrix products, arithmetic and copies ran while one was open for 3% of the time, Pallas kernels for 7%

profile of v1, /device:TPU:1, one launch (start us, length us, event | category | flops | bytes accessed | tf_op | source)
XLA Modules:
  0.0 427.2 jit_solution(12102313187650021687)
XLA Ops:
  9.1 22.0 %all_to_all.25 = bf16[8,20,3072]{2,1,0:T(8,128)(2,1)S(1)} all-to-all(bf16[8,20,3072]{2,1,0:T(8,128)(2,1)S(1)} %broadcast_in_dim.38), channel_id=1, replica_groups=mesh['yh'=2,'z'=4,'core'=2,'yl'=2,'x'=4] {'yl','x'}, dimensions={0} | all-to-all | bytes 1966080 | tf_op jit(solution)/shard_map/all_to_all | solution.py:127
  34.2 4.2 collective-permute-start
  39.4 84.8 %collective-permute-done.other_up = bf16[2560,1536]{1,0:T(8,128)(2,1)} collective-permute-done((bf16[2560,1536]{1,0:T(8,128)(2,1)}, bf16[2560,1536]{1,0:T(8,128)(2,1)}, u32[]{:S(2)}, u32[]{:S(2)}) %collective-permute-start) | collective-permute-done | bytes 7864352 | tf_op jit(solution)/shard_map/ppermute | solution.py:251
  124.2 3.6 copy-done.1
  127.8 1.9 shard_map.130
  129.6 3.6 all-to-all-start.1
  133.2 3.9 fusion.projected
  137.1 11.9 %all-to-all-done.1 = bf16[8,128,512]{2,1,0:T(8,128)(2,1)S(1)} async-done(((bf16[8,128,512]{2,1,0:T(8,128)(2,1)}), bf16[8,128,512]{2,1,0:T(8,128)(2,1)S(1)}, u32[]{:S(2)}, u32[]{:S(2)}) %all-to-all-start.1) | async-done | bytes 1048608 | tf_op jit(solution)/shard_map/all_to_all | solution.py:293
  149.0 3.2 collective-permute-start.1
  153.0 4.1 shard_map.131
  157.1 23.2 %all-gather.5.cloned.1.call-done = bf16[1280,2560]{1,0:T(8,128)(2,1)} async-done(((bf16[80,2560]{1,0:T(8,128)(2,1)}), bf16[1280,2560]{1,0:T(8,128)(2,1)}) %all-gather.5.cloned.1.call-update) | async-done | bytes 6553616 | tf_op jit(solution)/shard_map/all_gather | solution.py:255
  180.4 4.0 multiply_reduce_fusion
  186.0 10.3 %collective-permute-done.1.other_down = bf16[768,2560]{1,0:T(8,128)(2,1)} collective-permute-done((bf16[768,2560]{1,0:T(8,128)(2,1)}, bf16[768,2560]{1,0:T(8,128)(2,1)}, u32[]{:S(2)}, u32[]{:S(2)}) %collective-permute-start.1) | collective-permute-done | bytes 3932192 | tf_op jit(solution)/shard_map/ppermute | solution.py:296
  196.4 77.0 %all_to_all.26 = bf16[64,16,2560]{2,1,0:T(8,128)(2,1)} all-to-all(bf16[64,16,2560]{2,1,0:T(8,128)(2,1)S(1)} %bitcast.51), channel_id=1, replica_groups=mesh['yh'=2,'z'=4,'core'=2,'yl'=2,'x'=4] {'yh','z','yl','x'}, dimensions={0} | all-to-all | bytes 10485760 | tf_op jit(solution)/shard_map/all_to_all | solution.py:306
  274.8 2.1 copy-done
  276.9 11.8 %shard_map.132.rest_0_ = bf16[1024,2560]{1,0:T(8,128)(2,1)} custom-call(s32[1]{0:T(128)} %bitcast.12.keep, bf16[1024,2560]{1,0:T(8,128)(2,1)} %bitcast.14.rows, bf16[2560,1536]{1,0:T(8,128)(2,1)} %bitcast.53, bf16[2560,1536]{1,0:T(8,128)(2,1)} %collective-permute-done.other_up, bf16[768,2560]{1,0:T(8,128)(2,1)S(1)} %bitcast.44, ...), custom_call_target="tpu_custom_call" | custom-call | flops 6039797760 | bytes 17039360 | tf_op jit(solution)/shard_map/pallas_call | solution.py:190
  288.7 18.3 %shard_map.134 = bf16[1024,2560]{1,0:T(8,128)(2,1)} custom-call(s32[1]{0:T(128)} %bitcast.12.keep, bf16[1024,2560]{1,0:T(8,128)(2,1)} %collective-permute-done.2.rows, bf16[2560,1536]{1,0:T(8,128)(2,1)} %bitcast.54, bf16[2560,1536]{1,0:T(8,128)(2,1)} %collective-permute-done.other_up, bf16[768,2560]{1,0:T(8,128)(2,1)S(1)} %bitcast.45, ...), custom_call_target="tpu_custom_call" | custom-call | flops 12079595520 | bytes 22282240 | tf_op jit(solution)/shard_map/pallas_call | solution.py:190
  307.3 11.8 %shard_map.133 = bf16[1024,2560]{1,0:T(8,128)(2,1)} custom-call(s32[1]{0:T(128)} %bitcast.12.keep, bf16[1024,2560]{1,0:T(8,128)(2,1)} %bitcast.14.rows, bf16[2560,1536]{1,0:T(8,128)(2,1)} %bitcast.55, bf16[2560,1536]{1,0:T(8,128)(2,1)} %collective-permute-done.other_up, bf16[768,2560]{1,0:T(8,128)(2,1)S(1)} %bitcast.46, ...), custom_call_target="tpu_custom_call", output_to_operand_aliasing={{}: (6, {})} | custom-call | flops 6039797760 | bytes 17039360 | tf_op jit(solution)/shard_map/pallas_call | solution.py:190
  319.2 6.1 %add_convert_fusion = bf16[1024,2560]{1,0:T(8,128)(2,1)} fusion(bf16[1024,2560]{1,0:T(8,128)(2,1)S(1)} %collective-permute-done.3, bf16[1024,2560]{1,0:T(8,128)(2,1)} %shard_map.133), kind=kLoop, calls=%fused_computation | loop fusion | flops 10485760 | bytes 15728640 | tf_op jit(solution)/shard_map/convert_element_type | solution.py:318
  325.3 6.4 %all-to-all-start.3 = ((bf16[64,16,2560]{2,1,0:T(8,128)(2,1)}), bf16[64,16,2560]{2,1,0:T(8,128)(2,1)}, u32[]{:S(2)}, u32[]{:S(2)}) async-start(bf16[64,16,2560]{2,1,0:T(8,128)(2,1)} %bitcast.56), calls=%async_computation.3 | async-start | bytes 10485760 | tf_op jit(solution)/shard_map/all_to_all | solution.py:319
  331.9 69.9 %all-to-all-done.3 = bf16[64,16,2560]{2,1,0:T(8,128)(2,1)} async-done(((bf16[64,16,2560]{2,1,0:T(8,128)(2,1)}), bf16[64,16,2560]{2,1,0:T(8,128)(2,1)}, u32[]{:S(2)}, u32[]{:S(2)}) %all-to-all-start.3) | async-done | bytes 5242912 | tf_op jit(solution)/shard_map/all_to_all | solution.py:319
  401.8 4.2 fusion.13
  407.1 3.5 all-to-all-start.4
  411.8 7.4 %all-to-all-done.4 = bf16[8,16,2560]{2,1,0:T(8,128)(2,1)S(1)} async-done(((bf16[8,16,2560]{2,1,0:T(8,128)(2,1)}), bf16[8,16,2560]{2,1,0:T(8,128)(2,1)S(1)}, u32[]{:S(2)}, u32[]{:S(2)}) %all-to-all-start.4) | async-done | bytes 655392 | tf_op jit(solution)/shard_map/all_to_all | solution.py:328
  (68 shorter events, 13.5 us)
Async XLA Ops:
  7.2 117.0 %all-gather.3.cloned.1.call-start = ((), (), s32[]{:S(2)}) async-start(), calls=%async_computation.5 | async-start | bytes 9748480 | tf_op jit(solution)/shard_map/all_gather | solution.py:254
  31.2 7.2 %copy-start.2 = (s32[1024]{0:T(1024)S(1)}, s32[1024]{0:T(1024)}, u32[]{:S(2)}) copy-start(s32[1024]{0:T(1024)} %param.12) | copy-start | bytes 12292
  31.2 7.2 %copy-start.10 = (s32[128]{0:T(128)S(1)}, s32[128]{0:T(128)}, u32[]{:S(2)}) copy-start(s32[128]{0:T(128)} %param.13) | copy-start | bytes 1540
  31.2 7.7 %copy-start.5 = (bf16[128,2560]{1,0:T(8,128)(2,1)S(1)}, bf16[128,2560]{1,0:T(8,128)(2,1)}, u32[]{:S(2)}) copy-start(bf16[128,2560]{1,0:T(8,128)(2,1)} %param.11) | copy-start | bytes 1966084
  32.1 7.0 %copy-start.6 = (f32[2560]{0:T(1024)S(1)}, f32[2560]{0:T(1024)}, u32[]{:S(2)}) copy-start(f32[2560]{0:T(1024)} %param.14) | copy-start | bytes 30724
  33.4 146.9 %all-gather.5.cloned.1.call-start = ((), (), s32[]{:S(2)}) async-start(), calls=%async_computation.6 | async-start | bytes 6963200 | tf_op jit(solution)/shard_map/all_gather | solution.py:255
  34.2 90.0 %collective-permute-start = (bf16[2560,1536]{1,0:T(8,128)(2,1)}, bf16[2560,1536]{1,0:T(8,128)(2,1)}, u32[]{:S(2)}, u32[]{:S(2)}) collective-permute-start(bf16[2560,1536]{1,0:T(8,128)(2,1)} %bitcast.52), channel_id=1, source_target_pairs={{8,1},{1,8},{10,3},{3,10},{12,5},{5,12},{14,7},{7,14},{24,17},{17,... | collective-permute-start | bytes 23592968 | tf_op jit(solution)/shard_map/ppermute | solution.py:251
  124.2 3.6 copy-start.1
  129.6 19.4 %all-to-all-start.1 = ((bf16[8,128,512]{2,1,0:T(8,128)(2,1)}), bf16[8,128,512]{2,1,0:T(8,128)(2,1)S(1)}, u32[]{:S(2)}, u32[]{:S(2)}) async-start(bf16[8,128,512]{2,1,0:T(8,128)(2,1)} %shard_map.130), calls=%async_computation.1 | async-start | bytes 2097152 | tf_op jit(solution)/shard_map/all_to_all | solution.py:293
  133.2 19.4 %copy-start.9 = (s32[128,6]{0,1:T(8,128)S(1)}, s32[128,6]{0,1:T(8,128)}, u32[]{:S(2)}) copy-start(s32[128,6]{0,1:T(8,128)} %param.18) | copy-start | bytes 9220
  149.0 47.3 %collective-permute-start.1 = (bf16[768,2560]{1,0:T(8,128)(2,1)}, bf16[768,2560]{1,0:T(8,128)(2,1)}, u32[]{:S(2)}, u32[]{:S(2)}) collective-permute-start(bf16[768,2560]{1,0:T(8,128)(2,1)} %bitcast.43), channel_id=1, source_target_pairs={{8,1},{1,8},{10,3},{3,10},{12,5},{5,12},{14,7},{7,14},{24,17},{17,... | collective-permute-start | bytes 11796488 | tf_op jit(solution)/shard_map/ppermute | solution.py:296
  157.1 27.2 %copy-start.7 = (f32[2560]{0:T(1024)S(1)}, f32[2560]{0:T(1024)}, u32[]{:S(2)}) copy-start(f32[2560]{0:T(1024)} %param.17) | copy-start | bytes 30724
  184.3 1.6 copy-start.3
  273.3 15.4 %collective-permute-start.2 = (bf16[1024,2560]{1,0:T(8,128)(2,1)}, bf16[1024,2560]{1,0:T(8,128)(2,1)}, u32[]{:S(2)}, u32[]{:S(2)}) collective-permute-start(bf16[1024,2560]{1,0:T(8,128)(2,1)} %bitcast.14.rows), channel_id=1, source_target_pairs={{0,8},{8,0},{1,9},{9,1},{2,10},{10,2},{3,11},{11,3},{4,12},{12,4},... | collective-permute-start | bytes 15728648 | tf_op jit(solution)/shard_map/ppermute | solution.py:309
  274.8 2.1 copy-start
  307.0 12.1 %collective-permute-start.3 = (bf16[1024,2560]{1,0:T(8,128)(2,1)}, bf16[1024,2560]{1,0:T(8,128)(2,1)S(1)}, u32[]{:S(2)}, u32[]{:S(2)}) collective-permute-start(bf16[1024,2560]{1,0:T(8,128)(2,1)} %shard_map.134), channel_id=1, source_target_pairs={{0,8},{8,0},{1,9},{9,1},{2,10},{10,2},{3,11},{11,3},{4,12},{12,4},... | collective-permute-start | bytes 15728648 | tf_op jit(solution)/shard_map/ppermute | solution.py:316
  325.3 6.4 %copy-start.8 = (f32[128,6]{0,1:T(8,128)S(1)}, f32[128,6]{0,1:T(8,128)}, u32[]{:S(2)}) copy-start(f32[128,6]{0,1:T(8,128)} %param.19) | copy-start | bytes 9220
  325.3 76.6 %all-to-all-start.3 = ((bf16[64,16,2560]{2,1,0:T(8,128)(2,1)}), bf16[64,16,2560]{2,1,0:T(8,128)(2,1)}, u32[]{:S(2)}, u32[]{:S(2)}) async-start(bf16[64,16,2560]{2,1,0:T(8,128)(2,1)} %bitcast.56), calls=%async_computation.3 | async-start | bytes 10485760 | tf_op jit(solution)/shard_map/all_to_all | solution.py:319
  401.8 4.2 copy-start.4
  407.1 12.1 %all-to-all-start.4 = ((bf16[8,16,2560]{2,1,0:T(8,128)(2,1)}), bf16[8,16,2560]{2,1,0:T(8,128)(2,1)S(1)}, u32[]{:S(2)}, u32[]{:S(2)}) async-start(bf16[8,16,2560]{2,1,0:T(8,128)(2,1)} %bitcast.17), calls=%async_computation.4 | async-start | bytes 1310720 | tf_op jit(solution)/shard_map/all_to_all | solution.py:328
Sparse Core Ops, SparseCore 0:
  33.5 78.3 all-gather.2
  114.4 65.8 all-gather.4

commit v2 on v1

--- a/solution.py
+++ b/solution.py
@@ -131,88 +131,37 @@
 
 CORES = [(0, 1), (1, 0)]
 ROW_TILE = 256
-UP_CHUNK = 640
-
-
-def expert_kernel(keep, rows, own_up, other_up, own_down, other_down, *rest):
-    out, up, down, up_sems, down_sem = rest[-5:]
-    up_chunks = up.shape[0] // UP_CHUNK
+
+
+def expert_kernel(rows, up, down, *rest):
+    out = rest[-1]
     half_size = up.shape[1] // 2
-
-    def up_copy(i, mine):
-        part = pl.ds(i * UP_CHUNK, UP_CHUNK)
-        source = own_up if mine else other_up
-        return pltpu.make_async_copy(source.at[part], up.at[part], up_sems.at[i])
-
-    def down_copy(mine):
-        return pltpu.make_async_copy(own_down if mine else other_down, down, down_sem)
-
-    def finish(joined, wait):
-        gate = joined[:, :half_size]
-        active = (gate / (1.0 + jnp.exp(-gate)) * joined[:, half_size:]).astype(jnp.bfloat16)
-        if wait:
-            down_copy(True).wait()
-        out[...] = jnp.dot(active, down[...], preferred_element_type=jnp.float32).astype(jnp.bfloat16)
-
-    @pl.when(pl.program_id(0) == 0)
-    def _():
-        @pl.when(keep[0] == 1)
-        def _():
-            for i in range(up_chunks):
-                up_copy(i, True).start()
-            down_copy(True).start()
-
-        @pl.when(keep[0] == 0)
-        def _():
-            for i in range(up_chunks):
-                up_copy(i, False).start()
-            down_copy(False).start()
-
-        joined = jnp.zeros((rows.shape[0], up.shape[1]), jnp.float32)
-        for i in range(up_chunks):
-            up_copy(i, True).wait()
-            part = slice(i * UP_CHUNK, (i + 1) * UP_CHUNK)
-            joined = joined + jnp.dot(
-                rows[:, part], up[part, :], preferred_element_type=jnp.float32
-            )
-        finish(joined, True)
-
-    @pl.when(pl.program_id(0) != 0)
-    def _():
-        finish(jnp.dot(rows[...], up[...], preferred_element_type=jnp.float32), False)
-
-
-def expert_half(keep, rows, weights, first, tiles, filled=None):
-    own_up, _, own_down, _ = weights
-    anywhere = pl.BlockSpec(memory_space=pl.ANY)
-    tile = pl.BlockSpec((ROW_TILE, rows.shape[1]), lambda i, keep: (first + i, 0))
+    joined = jnp.dot(rows[...], up[...], preferred_element_type=jnp.float32)
+    gate = joined[:, :half_size]
+    active = (gate / (1.0 + jnp.exp(-gate)) * joined[:, half_size:]).astype(jnp.bfloat16)
+    out[...] = jnp.dot(active, down[...], preferred_element_type=jnp.float32).astype(jnp.bfloat16)
+
+
+def expert_half(rows, up, down, first, tiles, filled=None):
+    kept = pl.BlockSpec(memory_space=pltpu.VMEM)
+    tile = pl.BlockSpec((ROW_TILE, rows.shape[1]), lambda i: (first + i, 0))
     extra = [] if filled is None else [filled]
     return pl.pallas_call(
         expert_kernel,
         out_shape=jax.ShapeDtypeStruct(rows.shape, jnp.bfloat16),
-        grid_spec=pltpu.PrefetchScalarGridSpec(
-            num_scalar_prefetch=1,
-            grid=(tiles,),
-            in_specs=[tile] + [anywhere] * (4 + len(extra)),
-            out_specs=tile,
-            scratch_shapes=[
-                pltpu.VMEM(own_up.shape, jnp.bfloat16),
-                pltpu.VMEM(own_down.shape, jnp.bfloat16),
-                pltpu.SemaphoreType.DMA((own_up.shape[0] // UP_CHUNK,)),
-                pltpu.SemaphoreType.DMA,
-            ],
-        ),
-        input_output_aliases={} if filled is None else {6: 0},
+        grid=(tiles,),
+        in_specs=[tile, kept, kept] + [pl.BlockSpec(memory_space=pl.ANY)] * len(extra),
+        out_specs=tile,
+        input_output_aliases={} if filled is None else {3: 0},
         compiler_params=pltpu.CompilerParams(
-            dimension_semantics=("arbitrary",), vmem_limit_bytes=50 << 20
+            dimension_semantics=("arbitrary",), vmem_limit_bytes=40 << 20
         ),
         cost_estimate=pl.CostEstimate(
-            flops=2 * tiles * ROW_TILE * (own_up.size + own_down.size),
-            transcendentals=tiles * ROW_TILE * own_down.shape[0],
-            bytes_accessed=2 * (own_up.size + own_down.size)
-            + 4 * tiles * ROW_TILE * rows.shape[1],
+            flops=2 * tiles * ROW_TILE * (up.size + down.size),
+            transcendentals=tiles * ROW_TILE * down.shape[0],
+            bytes_accessed=4 * tiles * ROW_TILE * rows.shape[1],
         ),
-    )(keep, rows, *weights, *extra)
+    )(rows, up, down, *extra)
 
 
 def per_device(
@@ -302,19 +251,20 @@
     moe_in = rms_scaled(attended, moe_gain)
 
     outgoing = jnp.dot(pick, moe_in, preferred_element_type=jnp.float32).astype(jnp.bfloat16)
-    outgoing, other_down = lax.optimization_barrier((outgoing, other_down))
+    outgoing, other_up, other_down = lax.optimization_barrier((outgoing, other_up, other_down))
+    up = jnp.where(keep, w_gate_up[0], other_up)
+    down = jnp.where(keep, w_down[0], other_down)
     mine = lax.all_to_all(
         outgoing.reshape(CHIP_COUNT, MOST, model_width), CHIPS, 0, 0, tiled=True
     ).reshape(CHIP_COUNT * MOST, model_width)
+    mine, up, down = lax.optimization_barrier((mine, up, down))
     mates = lax.ppermute(mine, "core", CORES)
-    weights = (w_gate_up[0], other_up, w_down[0], other_down)
-    kept = keep.astype(jnp.int32).reshape(1)
     tiles = mine.shape[0] // ROW_TILE
-    own_part = expert_half(kept, mine, weights, 0, tiles // 2)
+    own_part = expert_half(mine, up, down, 0, tiles // 2)
     mates, own_part = lax.optimization_barrier((mates, own_part))
-    for_mate = expert_half(kept, mates, weights, 0, tiles)
+    for_mate = expert_half(mates, up, down, 0, tiles)
     from_mate = lax.ppermute(for_mate, "core", CORES)
-    own_part = expert_half(kept, mine, weights, tiles // 2, tiles // 2, own_part)
+    own_part = expert_half(mine, up, down, tiles // 2, tiles // 2, own_part)
     expert_out = (own_part.astype(jnp.float32) + from_mate.astype(jnp.float32)).astype(jnp.bfloat16)
     returned = lax.all_to_all(
         expert_out.reshape(CHIP_COUNT, MOST, model_width), CHIPS, 0, 0, tiled=True

time: 432 us -> 444 us (1.028)
  blocking collectives: 99 us -> 22 us
  waiting for transfers between devices: 208 us -> 267 us
  other arithmetic: 10.4 us -> 25.5 us
  starting transfers between devices: 22.7 us -> 34.4 us
  local copies, waits for them, and re-layouts: 9.1 us -> 16 us
  Pallas kernels: 47.9 us -> 42.3 us
    all_to_all x1 -> x0, blocking collectives: 77 us -> none  [per_device(): lax.all_to_all(outgoing.reshape(CHIP_COUNT, MOST, model_width), CHIPS, 0,...]
    all_to_all x0 -> x1, waiting for transfers between devices: none -> 60.7 us  [per_device(): lax.all_to_all(outgoing.reshape(CHIP_COUNT, MOST, model_width), CHIPS, 0,...]
    select_n x0 -> x2, other arithmetic: none -> 15.1 us  [the longest x1 9.37 us: per_device(): up = jnp.where(keep, w_gate_up[0], other_up)]
    all_to_all x0 -> x1, starting transfers between devices: none -> 10.7 us  [per_device(): lax.all_to_all(outgoing.reshape(CHIP_COUNT, MOST, model_width), CHIPS, 0,...]
    pallas_call x3, Pallas kernels: 41.9 us -> 36.5 us  [expert_half(): pl.pallas_call(expert_kernel, out_shape=jax.ShapeDtypeStruct(rows.shape,...]
    unnamed x23 -> x29, local copies, waits for them, and re-layouts: 5.84 us -> 10.7 us
  transfers between devices with their start and end apart: 9 -> 10, of which waited for: 6 -> 7; matrix products, arithmetic and copies ran while one was open for 3% -> 7% of each run, Pallas kernels for 7% -> 6%
where the time goes in v2:
time: 444 us; the launch traced here: 439 us
  waiting for transfers between devices  267 us (60%)
  Pallas kernels  42.3 us (10%)
  starting transfers between devices  34.4 us (8%)
  other arithmetic  25.5 us (6%)
  blocking collectives  22 us (5%)
  matrix products  17.7 us (4%)
  local copies, waits for them, and re-layouts  16 us (4%)
  between operations  14.4 us (3%)
    ppermute x1, waiting for transfers between devices, per_device(): other_up = lax.ppermute(sent_up, ALL, pairs)  84.8 us
    all_to_all x1, waiting for transfers between devices, per_device(): lax.all_to_all(expert_out.reshape(CHIP_COUNT, MOST, model_width), CHIPS,...  69.9 us
    all_to_all x1, waiting for transfers between devices, per_device(): lax.all_to_all(outgoing.reshape(CHIP_COUNT, MOST, model_width), CHIPS, 0,...  60.7 us
    pallas_call x3, Pallas kernels, expert_half(): pl.pallas_call(expert_kernel, out_shape=jax.ShapeDtypeStruct(rows.shape,...  36.5 us
    all_gather x1, waiting for transfers between devices, per_device(): full_out = lax.all_gather(out_rows, DP, axis=0, tiled=True)  23.4 us
    all_to_all x1, blocking collectives, spread(): lax.all_to_all(jnp.broadcast_to(shard[None], (count,) + shard.shape), axe...  22 us
    all_to_all x1, waiting for transfers between devices, per_device(): lax.all_to_all(kv_copies, CACHE, 0, 0, tiled=True)  11.9 us
    all_to_all x1, starting transfers between devices, per_device(): lax.all_to_all(outgoing.reshape(CHIP_COUNT, MOST, model_width), CHIPS, 0,...  10.7 us
  transfers between devices with their start and end apart: 10, of which 7 were waited for; matrix products, arithmetic and copies ran while one was open for 7% of the time, Pallas kernels for 6%

profile of v2, /device:TPU:1, one launch (start us, length us, event | category | flops | bytes accessed | tf_op | source)
XLA Modules:
  0.0 439.2 jit_solution(13537844092161939631)
XLA Ops:
  9.1 22.0 %all_to_all.25 = bf16[8,20,3072]{2,1,0:T(8,128)(2,1)S(1)} all-to-all(bf16[8,20,3072]{2,1,0:T(8,128)(2,1)S(1)} %broadcast_in_dim.38), channel_id=1, replica_groups=mesh['yh'=2,'z'=4,'core'=2,'yl'=2,'x'=4] {'yl','x'}, dimensions={0} | all-to-all | bytes 1966080 | tf_op jit(solution)/shard_map/all_to_all | solution.py:127
  36.1 4.2 collective-permute-start
  41.3 84.8 %collective-permute-done = bf16[2560,1536]{1,0:T(8,128)(2,1)} collective-permute-done((bf16[2560,1536]{1,0:T(8,128)(2,1)}, bf16[2560,1536]{1,0:T(8,128)(2,1)}, u32[]{:S(2)}, u32[]{:S(2)}) %collective-permute-start) | collective-permute-done | bytes 7864352 | tf_op jit(solution)/shard_map/ppermute | solution.py:200
  126.1 3.6 copy-done.2
  131.7 3.6 all-to-all-start.1
  135.2 3.9 fusion.projected
  139.2 11.9 %all-to-all-done.1 = bf16[8,128,512]{2,1,0:T(8,128)(2,1)S(1)} async-done(((bf16[8,128,512]{2,1,0:T(8,128)(2,1)}), bf16[8,128,512]{2,1,0:T(8,128)(2,1)S(1)}, u32[]{:S(2)}, u32[]{:S(2)}) %all-to-all-start.1) | async-done | bytes 1048608 | tf_op jit(solution)/shard_map/all_to_all | solution.py:242
  155.0 3.9 shard_map.131
  158.9 23.4 %all-gather.5.cloned.1.call-done = bf16[1280,2560]{1,0:T(8,128)(2,1)} async-done(((bf16[80,2560]{1,0:T(8,128)(2,1)}), bf16[1280,2560]{1,0:T(8,128)(2,1)}) %all-gather.5.cloned.1.call-update) | async-done | bytes 6553616 | tf_op jit(solution)/shard_map/all_gather | solution.py:204
  182.3 4.1 multiply_reduce_fusion
  186.4 4.0 convolution_convert_fusion
  190.4 7.9 %collective-permute-done.1 = bf16[768,2560]{1,0:T(8,128)(2,1)} collective-permute-done((bf16[768,2560]{1,0:T(8,128)(2,1)}, bf16[768,2560]{1,0:T(8,128)(2,1)}, u32[]{:S(2)}, u32[]{:S(2)}) %collective-permute-start.1) | collective-permute-done | bytes 3932192 | tf_op jit(solution)/shard_map/ppermute | solution.py:245
  198.4 10.7 %all-to-all-start.2 = ((bf16[64,16,2560]{2,1,0:T(8,128)(2,1)}), bf16[64,16,2560]{2,1,0:T(8,128)(2,1)}, u32[]{:S(2)}, u32[]{:S(2)}) async-start(bf16[64,16,2560]{2,1,0:T(8,128)(2,1)} %bitcast.48), calls=%async_computation.2 | async-start | bytes 10485760 | tf_op jit(solution)/shard_map/all_to_all | solution.py:257
  209.1 5.7 %broadcast_select_fusion.1.down = bf16[768,2560]{1,0:T(8,128)(2,1)} fusion(bf16[768,2560]{1,0:T(8,128)(2,1)} %collective-permute-done.1, pred[]{:T(512)S(6)} %eq.80, bf16[1,768,2560]{2,1,0:T(8,128)(2,1)} %param.21), kind=kLoop, calls=%fused_computation.5 | loop fusion | flops 1966080 | bytes 11796481 | tf_op jit(solution)/shard_map/jit(_where)/select_n | solution.py:256
  214.8 9.4 %broadcast_select_fusion.up = bf16[2560,1536]{1,0:T(8,128)(2,1)} fusion(bf16[2560,1536]{1,0:T(8,128)(2,1)} %collective-permute-done, pred[]{:T(512)S(6)} %eq.80, bf16[1,2560,1536]{2,1,0:T(8,128)(2,1)} %param.20), kind=kLoop, calls=%fused_computation.1 | loop fusion | flops 3932160 | bytes 23592960 | tf_op jit(solution)/shard_map/jit(_where)/select_n | solution.py:255
  224.2 60.7 %all-to-all-done.2 = bf16[64,16,2560]{2,1,0:T(8,128)(2,1)} async-done(((bf16[64,16,2560]{2,1,0:T(8,128)(2,1)}), bf16[64,16,2560]{2,1,0:T(8,128)(2,1)}, u32[]{:S(2)}, u32[]{:S(2)}) %all-to-all-start.2) | async-done | bytes 5242912 | tf_op jit(solution)/shard_map/all_to_all | solution.py:257
  288.0 10.2 %shard_map.132.rest_0_ = bf16[1024,2560]{1,0:T(8,128)(2,1)S(1)} custom-call(bf16[1024,2560]{1,0:T(8,128)(2,1)} %bitcast.13.rows, bf16[2560,1536]{1,0:T(8,128)(2,1)} %broadcast_select_fusion.up, bf16[768,2560]{1,0:T(8,128)(2,1)S(1)} %copy-done), custom_call_target="tpu_custom_call" | custom-call | flops 6039797760 | bytes 5242880 | tf_op jit(solution)/shard_map/pallas_call | solution.py:149
  303.2 16.1 %shard_map.134 = bf16[1024,2560]{1,0:T(8,128)(2,1)S(1)} custom-call(bf16[1024,2560]{1,0:T(8,128)(2,1)S(1)} %copy-done.5, bf16[2560,1536]{1,0:T(8,128)(2,1)} %broadcast_select_fusion.up, bf16[768,2560]{1,0:T(8,128)(2,1)S(1)} %copy-done.1), custom_call_target="tpu_custom_call" | custom-call | flops 12079595520 | bytes 10485760 | tf_op jit(solution)/shard_map/pallas_call | solution.py:149
  319.4 10.1 %shard_map.133 = bf16[1024,2560]{1,0:T(8,128)(2,1)S(1)} custom-call(bf16[1024,2560]{1,0:T(8,128)(2,1)} %bitcast.13.rows, bf16[2560,1536]{1,0:T(8,128)(2,1)} %broadcast_select_fusion.up, bf16[768,2560]{1,0:T(8,128)(2,1)S(1)} %copy-done.1, bf16[1024,2560]{1,0:T(8,128)(2,1)S(1)} %shard_map.132.rest_0_), custom_call_target="tpu_custom_call", output_to_operand_aliasing={{}: (3, {})} | custom-call | flops 6039797760 | bytes 5242880 | tf_op jit(solution)/shard_map/pallas_call | solution.py:149
  329.5 6.2 %add_convert_fusion = bf16[1024,2560]{1,0:T(8,128)(2,1)} fusion(bf16[1024,2560]{1,0:T(8,128)(2,1)} %collective-permute-done.3, bf16[1024,2560]{1,0:T(8,128)(2,1)S(1)} %shard_map.133), kind=kLoop, calls=%fused_computation | loop fusion | flops 10485760 | bytes 15728640 | tf_op jit(solution)/shard_map/convert_element_type | solution.py:268
  335.7 8.0 %all-to-all-start.3 = ((bf16[64,16,2560]{2,1,0:T(8,128)(2,1)}), bf16[64,16,2560]{2,1,0:T(8,128)(2,1)}, u32[]{:S(2)}, u32[]{:S(2)}) async-start(bf16[64,16,2560]{2,1,0:T(8,128)(2,1)} %bitcast.49), calls=%async_computation.3 | async-start | bytes 10485760 | tf_op jit(solution)/shard_map/all_to_all | solution.py:269
  344.0 69.9 %all-to-all-done.3 = bf16[64,16,2560]{2,1,0:T(8,128)(2,1)} async-done(((bf16[64,16,2560]{2,1,0:T(8,128)(2,1)}), bf16[64,16,2560]{2,1,0:T(8,128)(2,1)}, u32[]{:S(2)}, u32[]{:S(2)}) %all-to-all-start.3) | async-done | bytes 5242912 | tf_op jit(solution)/shard_map/all_to_all | solution.py:269
  413.9 4.1 fusion.13
  423.7 7.4 %all-to-all-done.4 = bf16[8,16,2560]{2,1,0:T(8,128)(2,1)S(1)} async-done(((bf16[8,16,2560]{2,1,0:T(8,128)(2,1)}), bf16[8,16,2560]{2,1,0:T(8,128)(2,1)S(1)}, u32[]{:S(2)}, u32[]{:S(2)}) %all-to-all-start.4) | async-done | bytes 655392 | tf_op jit(solution)/shard_map/all_to_all | solution.py:278
  (77 shorter events, 28.9 us)
Async XLA Ops:
  7.2 119.0 %all-gather.3.cloned.1.call-start = ((), (), s32[]{:S(2)}) async-start(), calls=%async_computation.5 | async-start | bytes 9748480 | tf_op jit(solution)/shard_map/all_gather | solution.py:203
  32.0 8.3 %copy-start.3 = (s32[1024]{0:T(1024)S(1)}, s32[1024]{0:T(1024)}, u32[]{:S(2)}) copy-start(s32[1024]{0:T(1024)} %param.12) | copy-start | bytes 12292
  32.0 8.3 %copy-start.13 = (s32[128]{0:T(128)S(1)}, s32[128]{0:T(128)}, u32[]{:S(2)}) copy-start(s32[128]{0:T(128)} %param.13) | copy-start | bytes 1540
  32.0 8.9 %copy-start.8 = (bf16[128,2560]{1,0:T(8,128)(2,1)S(1)}, bf16[128,2560]{1,0:T(8,128)(2,1)}, u32[]{:S(2)}) copy-start(bf16[128,2560]{1,0:T(8,128)(2,1)} %param.11) | copy-start | bytes 1966084
  34.1 7.0 %copy-start.9 = (f32[2560]{0:T(1024)S(1)}, f32[2560]{0:T(1024)}, u32[]{:S(2)}) copy-start(f32[2560]{0:T(1024)} %param.14) | copy-start | bytes 30724
  35.4 147.0 %all-gather.5.cloned.1.call-start = ((), (), s32[]{:S(2)}) async-start(), calls=%async_computation.6 | async-start | bytes 6963200 | tf_op jit(solution)/shard_map/all_gather | solution.py:204
  36.1 90.0 %collective-permute-start = (bf16[2560,1536]{1,0:T(8,128)(2,1)}, bf16[2560,1536]{1,0:T(8,128)(2,1)}, u32[]{:S(2)}, u32[]{:S(2)}) collective-permute-start(bf16[2560,1536]{1,0:T(8,128)(2,1)} %bitcast.50), channel_id=1, source_target_pairs={{8,1},{1,8},{10,3},{3,10},{12,5},{5,12},{14,7},{7,14},{24,17},{17,... | collective-permute-start | bytes 23592968 | tf_op jit(solution)/shard_map/ppermute | solution.py:200
  126.1 3.6 copy-start.2
  131.7 19.4 %all-to-all-start.1 = ((bf16[8,128,512]{2,1,0:T(8,128)(2,1)}), bf16[8,128,512]{2,1,0:T(8,128)(2,1)S(1)}, u32[]{:S(2)}, u32[]{:S(2)}) async-start(bf16[8,128,512]{2,1,0:T(8,128)(2,1)} %shard_map.130), calls=%async_computation.1 | async-start | bytes 2097152 | tf_op jit(solution)/shard_map/all_to_all | solution.py:242
  135.2 19.4 %copy-start.12 = (s32[128,6]{0,1:T(8,128)S(1)}, s32[128,6]{0,1:T(8,128)}, u32[]{:S(2)}) copy-start(s32[128,6]{0,1:T(8,128)} %param.18) | copy-start | bytes 9220
  151.0 47.3 %collective-permute-start.1 = (bf16[768,2560]{1,0:T(8,128)(2,1)}, bf16[768,2560]{1,0:T(8,128)(2,1)}, u32[]{:S(2)}, u32[]{:S(2)}) collective-permute-start(bf16[768,2560]{1,0:T(8,128)(2,1)} %bitcast.51), channel_id=1, source_target_pairs={{8,1},{1,8},{10,3},{3,10},{12,5},{5,12},{14,7},{7,14},{24,17},{17,... | collective-permute-start | bytes 11796488 | tf_op jit(solution)/shard_map/ppermute | solution.py:245
  158.9 27.5 %copy-start.10 = (f32[2560]{0:T(1024)S(1)}, f32[2560]{0:T(1024)}, u32[]{:S(2)}) copy-start(f32[2560]{0:T(1024)} %param.17) | copy-start | bytes 30724
  186.4 4.0 copy-start.6
  198.4 86.5 %all-to-all-start.2 = ((bf16[64,16,2560]{2,1,0:T(8,128)(2,1)}), bf16[64,16,2560]{2,1,0:T(8,128)(2,1)}, u32[]{:S(2)}, u32[]{:S(2)}) async-start(bf16[64,16,2560]{2,1,0:T(8,128)(2,1)} %bitcast.48), calls=%async_computation.2 | async-start | bytes 10485760 | tf_op jit(solution)/shard_map/all_to_all | solution.py:257
  284.9 13.4 %collective-permute-start.2 = (bf16[1024,2560]{1,0:T(8,128)(2,1)}, bf16[1024,2560]{1,0:T(8,128)(2,1)S(1)}, u32[]{:S(2)}, u32[]{:S(2)}) collective-permute-start(bf16[1024,2560]{1,0:T(8,128)(2,1)} %bitcast.13.rows), channel_id=1, source_target_pairs={{0,8},{8,0},{1,9},{9,1},{2,10},{10,2},{3,11},{11,3},{4,12},{12,4},... | collective-permute-start | bytes 15728648 | tf_op jit(solution)/shard_map/ppermute | solution.py:261
  285.9 2.1 copy-start
  288.0 12.6 %copy-start.1 = (bf16[768,2560]{1,0:T(8,128)(2,1)S(1)}, bf16[768,2560]{1,0:T(8,128)(2,1)}, u32[]{:S(2)}) copy-start(bf16[768,2560]{1,0:T(8,128)(2,1)} %broadcast_select_fusion.1.down) | copy-start | bytes 11796484
  298.3 2.4 copy-start.4
  300.7 2.5 copy-start.5
  319.3 10.2 %collective-permute-start.3 = (bf16[1024,2560]{1,0:T(8,128)(2,1)S(1)}, bf16[1024,2560]{1,0:T(8,128)(2,1)}, u32[]{:S(2)}, u32[]{:S(2)}) collective-permute-start(bf16[1024,2560]{1,0:T(8,128)(2,1)S(1)} %shard_map.134), channel_id=1, source_target_pairs={{0,8},{8,0},{1,9},{9,1},{2,10},{10,2},{3,11},{11,3},{4,12},{12,4},... | collective-permute-start | bytes 15728648 | tf_op jit(solution)/shard_map/ppermute | solution.py:266
  335.7 8.0 %copy-start.11 = (f32[128,6]{0,1:T(8,128)S(1)}, f32[128,6]{0,1:T(8,128)}, u32[]{:S(2)}) copy-start(f32[128,6]{0,1:T(8,128)} %param.19) | copy-start | bytes 9220
  335.7 78.2 %all-to-all-start.3 = ((bf16[64,16,2560]{2,1,0:T(8,128)(2,1)}), bf16[64,16,2560]{2,1,0:T(8,128)(2,1)}, u32[]{:S(2)}, u32[]{:S(2)}) async-start(bf16[64,16,2560]{2,1,0:T(8,128)(2,1)} %bitcast.49), calls=%async_computation.3 | async-start | bytes 10485760 | tf_op jit(solution)/shard_map/all_to_all | solution.py:269
  413.9 4.1 copy-start.7
  419.0 12.1 %all-to-all-start.4 = ((bf16[8,16,2560]{2,1,0:T(8,128)(2,1)}), bf16[8,16,2560]{2,1,0:T(8,128)(2,1)S(1)}, u32[]{:S(2)}, u32[]{:S(2)}) async-start(bf16[8,16,2560]{2,1,0:T(8,128)(2,1)} %bitcast.16), calls=%async_computation.4 | async-start | bytes 1310720 | tf_op jit(solution)/shard_map/all_to_all | solution.py:278
Sparse Core Ops, SparseCore 0:
  35.5 78.3 all-gather.2
  116.4 65.9 all-gather.4

commit v3 on v1

--- a/solution.py
+++ b/solution.py
@@ -51,43 +51,22 @@
     return (head * cosines + pltpu.roll(head, HD // 2, 1) * sines).astype(jnp.bfloat16)
 
 
-def keys_values_kernel(normed, w_block, cosines, sines, out):
-    block = jnp.dot(normed[...], w_block[...], preferred_element_type=jnp.float32)
-
-    def write(columns, part):
-        for copy in range(out.shape[0]):
-            out[copy, :, columns] = part
-
-    @pl.when(pl.program_id(0) == 0)
-    def _():
-        for k in range(KVH):
-            columns = slice(k * HD, (k + 1) * HD)
-            write(columns, turned(block[:, columns], cosines[...], sines[...]))
-
-    @pl.when(pl.program_id(0) == 1)
-    def _():
-        write(slice(0, KVH * HD), block.astype(jnp.bfloat16))
-
-
-def keys_values(normed, w_qkv, cosines, sines, copies):
-    row_count, model_width = normed.shape
-    width = KVH * HD
-    whole = lambda i: (0, 0)
+def keys_values_kernel(projected, cosines, sines, out):
+    for k in range(2 * KVH):
+        columns = slice(k * HD, (k + 1) * HD)
+        if k < KVH:
+            part = turned(projected[:, columns], cosines[...], sines[...])
+        else:
+            part = projected[:, columns].astype(jnp.bfloat16)
+        for device in range(out.shape[0]):
+            out[device, :, columns] = part
+
+
+def keys_values(projected, cosines, sines, copies):
     return pl.pallas_call(
         keys_values_kernel,
-        out_shape=jax.ShapeDtypeStruct((copies, row_count, 2 * width), jnp.bfloat16),
-        grid=(2,),
-        in_specs=[
-            pl.BlockSpec((row_count, model_width), whole),
-            pl.BlockSpec((model_width, width), lambda i: (0, QH * HD // width + i)),
-            pl.BlockSpec((row_count, HD), whole),
-            pl.BlockSpec((row_count, HD), whole),
-        ],
-        out_specs=pl.BlockSpec((copies, row_count, width), lambda i: (0, 0, i)),
-        compiler_params=pltpu.CompilerParams(
-            dimension_semantics=("arbitrary",), vmem_limit_bytes=32 << 20
-        ),
-    )(normed, w_qkv, cosines, sines)
+        out_shape=jax.ShapeDtypeStruct((copies,) + projected.shape, jnp.bfloat16),
+    )(projected, cosines, sines)
 
 
 def attention_kernel(projected, cosines, sines, kv_group, placing, start, place, out):
@@ -134,8 +113,8 @@
 UP_CHUNK = 640
 
 
-def expert_kernel(keep, rows, own_up, other_up, own_down, other_down, *rest):
-    out, up, down, up_sems, down_sem = rest[-5:]
+def expert_kernel(keep, rows, own_up, other_up, own_down, other_first, other_second, *rest):
+    out, up, down, up_sems, down_sems = rest[-5:]
     up_chunks = up.shape[0] // UP_CHUNK
     half_size = up.shape[1] // 2
 
@@ -144,14 +123,19 @@
         source = own_up if mine else other_up
         return pltpu.make_async_copy(source.at[part], up.at[part], up_sems.at[i])
 
-    def down_copy(mine):
-        return pltpu.make_async_copy(own_down if mine else other_down, down, down_sem)
+    down_half = down.shape[0] // 2
+
+    def down_copy(i, mine):
+        part = pl.ds(i * down_half, down_half)
+        source = own_down.at[part] if mine else (other_first, other_second)[i]
+        return pltpu.make_async_copy(source, down.at[part], down_sems.at[i])
 
     def finish(joined, wait):
         gate = joined[:, :half_size]
         active = (gate / (1.0 + jnp.exp(-gate)) * joined[:, half_size:]).astype(jnp.bfloat16)
         if wait:
-            down_copy(True).wait()
+            for i in range(2):
+                down_copy(i, True).wait()
         out[...] = jnp.dot(active, down[...], preferred_element_type=jnp.float32).astype(jnp.bfloat16)
 
     @pl.when(pl.program_id(0) == 0)
@@ -160,13 +144,15 @@
         def _():
             for i in range(up_chunks):
                 up_copy(i, True).start()
-            down_copy(True).start()
+            for i in range(2):
+                down_copy(i, True).start()
 
         @pl.when(keep[0] == 0)
         def _():
             for i in range(up_chunks):
                 up_copy(i, False).start()
-            down_copy(False).start()
+            for i in range(2):
+                down_copy(i, False).start()
 
         joined = jnp.zeros((rows.shape[0], up.shape[1]), jnp.float32)
         for i in range(up_chunks):
@@ -183,8 +169,8 @@
 
 
 def expert_half(keep, rows, weights, first, tiles, filled=None):
-    own_up, _, own_down, _ = weights
-    anywhere = pl.BlockSpec(memory_space=pl.ANY)
+    own_up, _, own_down, _, _ = weights
+    anywhere = pl.BlockSpec(memory_space=pltpu.HBM)
     tile = pl.BlockSpec((ROW_TILE, rows.shape[1]), lambda i, keep: (first + i, 0))
     extra = [] if filled is None else [filled]
     return pl.pallas_call(
@@ -193,18 +179,18 @@
         grid_spec=pltpu.PrefetchScalarGridSpec(
             num_scalar_prefetch=1,
             grid=(tiles,),
-            in_specs=[tile] + [anywhere] * (4 + len(extra)),
+            in_specs=[tile] + [anywhere] * 5 + [pl.BlockSpec(memory_space=pl.ANY)] * len(extra),
             out_specs=tile,
             scratch_shapes=[
                 pltpu.VMEM(own_up.shape, jnp.bfloat16),
                 pltpu.VMEM(own_down.shape, jnp.bfloat16),
                 pltpu.SemaphoreType.DMA((own_up.shape[0] // UP_CHUNK,)),
-                pltpu.SemaphoreType.DMA,
+                pltpu.SemaphoreType.DMA((2,)),
             ],
         ),
-        input_output_aliases={} if filled is None else {6: 0},
+        input_output_aliases={} if filled is None else {7: 0},
         compiler_params=pltpu.CompilerParams(
-            dimension_semantics=("arbitrary",), vmem_limit_bytes=50 << 20
+            dimension_semantics=("arbitrary",), vmem_limit_bytes=60 << 20
         ),
         cost_estimate=pl.CostEstimate(
             flops=2 * tiles * ROW_TILE * (own_up.size + own_down.size),
@@ -247,8 +233,12 @@
     out_rows = jnp.concatenate([halves[:, 0], halves[:, 1]], axis=2).reshape(-1, w_out.shape[1])
 
     pairs = swap_pairs()
-    sent_up, qkv_rows, out_rows = lax.optimization_barrier((w_gate_up[0], qkv_rows, out_rows))
+    down_half = w_down.shape[1] // 2
+    sent_up, sent_first, qkv_rows, out_rows = lax.optimization_barrier(
+        (w_gate_up[0], w_down[0, :down_half], qkv_rows, out_rows)
+    )
     other_up = lax.ppermute(sent_up, ALL, pairs)
+    other_first = lax.ppermute(sent_first, ALL, pairs)
     keep = lax.axis_index("x") % 2 == lax.axis_index("core")
 
     full_qkv = lax.all_gather(qkv_rows, DP, axis=0, tiled=True)
@@ -289,11 +279,14 @@
     sine_part = jnp.sin(angles)
     cosines = jnp.concatenate([cosine, cosine], axis=1)
     sines = jnp.concatenate([-sine_part, sine_part], axis=1)
-    kv_copies = keys_values(normed, full_qkv, cosines, sines, cache_size)
+    kv_projected = jnp.dot(normed, full_qkv[:, query_width:], preferred_element_type=jnp.float32)
+    kv_copies = keys_values(kv_projected, cosines, sines, cache_size)
     kv_group = lax.all_to_all(kv_copies, CACHE, 0, 0, tiled=True).reshape(group_rows, 2 * kv_width)
     projected = jnp.dot(normed, full_qkv[:, :query_width], preferred_element_type=jnp.float32)
-    kv_group, projected, sent_down = lax.optimization_barrier((kv_group, projected, w_down[0]))
-    other_down = lax.ppermute(sent_down, ALL, pairs)
+    kv_group, projected, other_first, sent_second = lax.optimization_barrier(
+        (kv_group, projected, other_first, w_down[0, down_half:])
+    )
+    other_second = lax.ppermute(sent_second, ALL, pairs)
     context = attention(
         projected, cosines, sines, kv_group, placing[None, :], prompt_start[:, None], my_place[:, None]
     )
@@ -302,12 +295,12 @@
     moe_in = rms_scaled(attended, moe_gain)
 
     outgoing = jnp.dot(pick, moe_in, preferred_element_type=jnp.float32).astype(jnp.bfloat16)
-    outgoing, other_down = lax.optimization_barrier((outgoing, other_down))
+    outgoing, other_second = lax.optimization_barrier((outgoing, other_second))
     mine = lax.all_to_all(
         outgoing.reshape(CHIP_COUNT, MOST, model_width), CHIPS, 0, 0, tiled=True
     ).reshape(CHIP_COUNT * MOST, model_width)
     mates = lax.ppermute(mine, "core", CORES)
-    weights = (w_gate_up[0], other_up, w_down[0], other_down)
+    weights = (w_gate_up[0], other_up, w_down[0], other_first, other_second)
     kept = keep.astype(jnp.int32).reshape(1)
     tiles = mine.shape[0] // ROW_TILE
     own_part = expert_half(kept, mine, weights, 0, tiles // 2)

time: 432 us -> 416 us (0.963)
  blocking collectives: 99 us -> 70.5 us
  starting transfers between devices: 22.7 us -> 31.3 us
    all_to_all x1 -> x0, blocking collectives: 22 us -> none  [spread(): lax.all_to_all(jnp.broadcast_to(shard[None], (count,) + shard.shape), axe...]
    all_to_all x0 -> x1, waiting for transfers between devices: none -> 12.8 us  [spread(): lax.all_to_all(jnp.broadcast_to(shard[None], (count,) + shard.shape), axe...]
    all_gather x1, waiting for transfers between devices: 23.2 us -> 15.3 us  [per_device(): full_out = lax.all_gather(out_rows, DP, axis=0, tiled=True)]
    all_to_all x1, waiting for transfers between devices: 11.9 us -> 4.53 us  [per_device(): lax.all_to_all(kv_copies, CACHE, 0, 0, tiled=True)]
    all_to_all x1, blocking collectives: 77 us -> 70.5 us  [per_device(): lax.all_to_all(outgoing.reshape(CHIP_COUNT, MOST, model_width), CHIPS, 0,...]
    all_to_all x0 -> x1, starting transfers between devices: none -> 5.86 us  [spread(): lax.all_to_all(jnp.broadcast_to(shard[None], (count,) + shard.shape), axe...]
    unnamed x23, local copies, waits for them, and re-layouts: 5.84 us -> 0.13 us
    squeeze x0 -> x1, local copies, waits for them, and re-layouts: none -> 4.39 us  [per_device(): w_down[0, down_half:]]
  transfers between devices with their start and end apart: 9 -> 11, of which waited for: 6 -> 7; matrix products, arithmetic and copies ran while one was open for 3% -> 5% of each run, Pallas kernels for 7% -> 7%
where the time goes in v3:
time: 416 us; the launch traced here: 414 us
  waiting for transfers between devices  210 us (50%)
  blocking collectives  70.5 us (17%)
  Pallas kernels  48.3 us (12%)
  starting transfers between devices  31.3 us (8%)
  matrix products  18.4 us (4%)
  between operations  14.5 us (3%)
  other arithmetic  12.5 us (3%)
  local copies, waits for them, and re-layouts  8.85 us (2%)
    ppermute x1, waiting for transfers between devices, per_device(): other_up = lax.ppermute(sent_up, ALL, pairs)  82.5 us
    all_to_all x1, blocking collectives, per_device(): lax.all_to_all(outgoing.reshape(CHIP_COUNT, MOST, model_width), CHIPS, 0,...  70.5 us
    all_to_all x1, waiting for transfers between devices, per_device(): lax.all_to_all(expert_out.reshape(CHIP_COUNT, MOST, model_width), CHIPS,...  69.4 us
    pallas_call x3, Pallas kernels, expert_half(): pl.pallas_call(expert_kernel, out_shape=jax.ShapeDtypeStruct(rows.shape,...  42.1 us
    all_gather x1, waiting for transfers between devices, per_device(): full_out = lax.all_gather(out_rows, DP, axis=0, tiled=True)  15.3 us
    ppermute x1, waiting for transfers between devices, per_device(): other_first = lax.ppermute(sent_first, ALL, pairs)  14.2 us
    all_to_all x1, waiting for transfers between devices, spread(): lax.all_to_all(jnp.broadcast_to(shard[None], (count,) + shard.shape), axe...  12.8 us
    all_to_all x1, waiting for transfers between devices, per_device(): lax.all_to_all(finished.reshape(cache_size, deal_rows, model_width), CACH...  10.2 us
  transfers between devices with their start and end apart: 11, of which 7 were waited for; matrix products, arithmetic and copies ran while one was open for 5% of the time, Pallas kernels for 7%

profile of v3, /device:TPU:1, one launch (start us, length us, event | category | flops | bytes accessed | tf_op | source)
XLA Modules:
  0.0 413.9 jit_solution(10663487907032129671)
XLA Ops:
  10.1 5.9 %all-to-all-start = ((bf16[8,20,3072]{2,1,0:T(8,128)(2,1)}), bf16[8,20,3072]{2,1,0:T(8,128)(2,1)S(1)}, u32[]{:S(2)}, u32[]{:S(2)}) async-start(bf16[8,20,3072]{2,1,0:T(8,128)(2,1)} %broadcast_in_dim.38), calls=%async_computation | async-start | bytes 2359296 | tf_op jit(solution)/shard_map/all_to_all | solution.py:106
  16.0 4.4 %slice_bitcast_fusion = (bf16[384,2560]{1,0:T(8,128)(2,1)}, bf16[384,2560]{1,0:T(8,128)(2,1)}) fusion(bf16[1,768,2560]{2,1,0:T(8,128)(2,1)} %param.21), kind=kLoop, calls=%fused_computation.10 | loop fusion | bytes 7864320 | tf_op jit(solution)/shard_map/squeeze | solution.py:287
  20.4 12.8 %all-to-all-done = bf16[8,20,3072]{2,1,0:T(8,128)(2,1)S(1)} async-done(((bf16[8,20,3072]{2,1,0:T(8,128)(2,1)}), bf16[8,20,3072]{2,1,0:T(8,128)(2,1)S(1)}, u32[]{:S(2)}, u32[]{:S(2)}) %all-to-all-start) | async-done | bytes 983072 | tf_op jit(solution)/shard_map/all_to_all | solution.py:106
  36.2 3.2 collective-permute-start
  43.2 82.5 %collective-permute-done.other_up = bf16[2560,1536]{1,0:T(8,128)(2,1)} collective-permute-done((bf16[2560,1536]{1,0:T(8,128)(2,1)}, bf16[2560,1536]{1,0:T(8,128)(2,1)}, u32[]{:S(2)}, u32[]{:S(2)}) %collective-permute-start) | collective-permute-done | bytes 7864352 | tf_op jit(solution)/shard_map/ppermute | solution.py:240
  125.6 3.0 fusion.4.projected
  130.8 3.6 all-to-all-start.1
  134.4 4.0 fusion.projected
  138.4 14.2 %collective-permute-done.1.other_first = bf16[384,2560]{1,0:T(8,128)(2,1)} collective-permute-done((bf16[384,2560]{1,0:T(8,128)(2,1)}, bf16[384,2560]{1,0:T(8,128)(2,1)}, u32[]{:S(2)}, u32[]{:S(2)}) %collective-permute-start.1) | collective-permute-done | bytes 1966112 | tf_op jit(solution)/shard_map/ppermute | solution.py:241
  152.6 4.5 %all-to-all-done.1 = bf16[8,128,512]{2,1,0:T(8,128)(2,1)S(1)} async-done(((bf16[8,128,512]{2,1,0:T(8,128)(2,1)}), bf16[8,128,512]{2,1,0:T(8,128)(2,1)S(1)}, u32[]{:S(2)}, u32[]{:S(2)}) %all-to-all-start.1) | async-done | bytes 1048608 | tf_op jit(solution)/shard_map/all_to_all | solution.py:284
  157.1 4.4 %collective-permute-start.2 = (bf16[384,2560]{1,0:T(8,128)(2,1)}, bf16[384,2560]{1,0:T(8,128)(2,1)}, u32[]{:S(2)}, u32[]{:S(2)}) collective-permute-start(bf16[384,2560]{1,0:T(8,128)(2,1)} %get-tuple-element.24), channel_id=1, source_target_pairs={{8,1},{1,8},{10,3},{3,10},{12,5},{5,12},{14,7},{7,14},{24,17},{17,... | collective-permute-start | bytes 5898248 | tf_op jit(solution)/shard_map/ppermute | solution.py:289
  162.3 4.1 shard_map.131
  166.4 15.3 %all-gather.5.cloned.1.call-done = bf16[1280,2560]{1,0:T(8,128)(2,1)} async-done(((bf16[80,2560]{1,0:T(8,128)(2,1)}), bf16[1280,2560]{1,0:T(8,128)(2,1)}) %all-gather.5.cloned.1.call-update) | async-done | bytes 6553616 | tf_op jit(solution)/shard_map/all_gather | solution.py:245
  181.7 4.0 multiply_reduce_fusion
  187.4 70.5 %all_to_all.25 = bf16[64,16,2560]{2,1,0:T(8,128)(2,1)} all-to-all(bf16[64,16,2560]{2,1,0:T(8,128)(2,1)S(1)} %bitcast.50), channel_id=1, replica_groups=mesh['yh'=2,'z'=4,'core'=2,'yl'=2,'x'=4] {'yh','z','yl','x'}, dimensions={0} | all-to-all | bytes 10485760 | tf_op jit(solution)/shard_map/all_to_all | solution.py:299
  259.6 11.9 %shard_map.132.rest_0_ = bf16[1024,2560]{1,0:T(8,128)(2,1)} custom-call(s32[1]{0:T(128)} %bitcast.13.keep, bf16[1024,2560]{1,0:T(8,128)(2,1)} %bitcast.15.rows, bf16[2560,1536]{1,0:T(8,128)(2,1)} %bitcast.55, bf16[2560,1536]{1,0:T(8,128)(2,1)} %collective-permute-done.other_up, bf16[768,2560]{1,0:T(8,128)(2,1)} %bitcast.51, ...), custom_call_target="tpu_custom_call" | custom-call | flops 6039797760 | bytes 17039360 | tf_op jit(solution)/shard_map/pallas_call | solution.py:176
  271.5 18.3 %shard_map.134 = bf16[1024,2560]{1,0:T(8,128)(2,1)} custom-call(s32[1]{0:T(128)} %bitcast.13.keep, bf16[1024,2560]{1,0:T(8,128)(2,1)} %collective-permute-done.3.rows, bf16[2560,1536]{1,0:T(8,128)(2,1)} %bitcast.56, bf16[2560,1536]{1,0:T(8,128)(2,1)} %collective-permute-done.other_up, bf16[768,2560]{1,0:T(8,128)(2,1)} %bitcast.52, ...), custom_call_target="tpu_custom_call" | custom-call | flops 12079595520 | bytes 22282240 | tf_op jit(solution)/shard_map/pallas_call | solution.py:176
  290.2 11.8 %shard_map.133 = bf16[1024,2560]{1,0:T(8,128)(2,1)} custom-call(s32[1]{0:T(128)} %bitcast.13.keep, bf16[1024,2560]{1,0:T(8,128)(2,1)} %bitcast.15.rows, bf16[2560,1536]{1,0:T(8,128)(2,1)} %bitcast.57, bf16[2560,1536]{1,0:T(8,128)(2,1)} %collective-permute-done.other_up, bf16[768,2560]{1,0:T(8,128)(2,1)} %bitcast.53, ...), custom_call_target="tpu_custom_call", output_to_operand_aliasing={{}: (7, {})} | custom-call | flops 6039797760 | bytes 17039360 | tf_op jit(solution)/shard_map/pallas_call | solution.py:176
  302.1 7.8 %add_convert_fusion = bf16[1024,2560]{1,0:T(8,128)(2,1)} fusion(bf16[1024,2560]{1,0:T(8,128)(2,1)} %collective-permute-done.4, bf16[1024,2560]{1,0:T(8,128)(2,1)} %shard_map.133), kind=kLoop, calls=%fused_computation | loop fusion | flops 10485760 | bytes 15728640 | tf_op jit(solution)/shard_map/convert_element_type | solution.py:311
  309.8 5.8 %all-to-all-start.3 = ((bf16[64,16,2560]{2,1,0:T(8,128)(2,1)}), bf16[64,16,2560]{2,1,0:T(8,128)(2,1)}, u32[]{:S(2)}, u32[]{:S(2)}) async-start(bf16[64,16,2560]{2,1,0:T(8,128)(2,1)} %bitcast.58), calls=%async_computation.3 | async-start | bytes 10485760 | tf_op jit(solution)/shard_map/all_to_all | solution.py:312
  315.9 69.4 %all-to-all-done.3 = bf16[64,16,2560]{2,1,0:T(8,128)(2,1)} async-done(((bf16[64,16,2560]{2,1,0:T(8,128)(2,1)}), bf16[64,16,2560]{2,1,0:T(8,128)(2,1)}, u32[]{:S(2)}, u32[]{:S(2)}) %all-to-all-start.3) | async-done | bytes 5242912 | tf_op jit(solution)/shard_map/all_to_all | solution.py:312
  385.3 4.2 %fusion.15 = f32[256,2560]{1,0:T(8,128)S(1)} fusion(bf16[1024,2560]{1,0:T(8,128)(2,1)} %bitcast.18, bf16[1024,128]{1,0:T(8,128)(2,1)S(1)} %get-tuple-element.40, bf16[1024,128]{1,0:T(8,128)(2,1)S(1)} %get-tuple-element.39), kind=kOutput, calls=%fused_computation.30 | convolution fusion | flops 1343225856 | bytes 8388608 | tf_op jit(solution)/shard_map/dot_general | solution.py:315
  390.5 4.0 all-to-all-start.4
  395.6 10.2 %all-to-all-done.4 = bf16[8,16,2560]{2,1,0:T(8,128)(2,1)S(1)} async-done(((bf16[8,16,2560]{2,1,0:T(8,128)(2,1)}), bf16[8,16,2560]{2,1,0:T(8,128)(2,1)S(1)}, u32[]{:S(2)}, u32[]{:S(2)}) %all-to-all-start.4) | async-done | bytes 655392 | tf_op jit(solution)/shard_map/all_to_all | solution.py:321
  (72 shorter events, 19.7 us)
Async XLA Ops:
  10.1 23.1 %all-to-all-start = ((bf16[8,20,3072]{2,1,0:T(8,128)(2,1)}), bf16[8,20,3072]{2,1,0:T(8,128)(2,1)S(1)}, u32[]{:S(2)}, u32[]{:S(2)}) async-start(bf16[8,20,3072]{2,1,0:T(8,128)(2,1)} %broadcast_in_dim.38), calls=%async_computation | async-start | bytes 2359296 | tf_op jit(solution)/shard_map/all_to_all | solution.py:106
  15.9 109.7 %all-gather.3.cloned.1.call-start = ((), (), s32[]{:S(2)}) async-start(), calls=%async_computation.5 | async-start | bytes 9748480 | tf_op jit(solution)/shard_map/all_gather | solution.py:244
  34.2 5.2 %copy-start.2 = (s32[1024]{0:T(1024)S(1)}, s32[1024]{0:T(1024)}, u32[]{:S(2)}) copy-start(s32[1024]{0:T(1024)} %param.12) | copy-start | bytes 12292
  34.2 5.2 %copy-start.9 = (s32[128]{0:T(128)S(1)}, s32[128]{0:T(128)}, u32[]{:S(2)}) copy-start(s32[128]{0:T(128)} %param.13) | copy-start | bytes 1540
  34.3 8.7 %copy-start.5 = (bf16[128,2560]{1,0:T(8,128)(2,1)S(1)}, bf16[128,2560]{1,0:T(8,128)(2,1)}, u32[]{:S(2)}) copy-start(bf16[128,2560]{1,0:T(8,128)(2,1)} %param.11) | copy-start | bytes 1966084
  34.3 91.3 %copy-start.10 = (f32[2560]{0:T(1024)S(1)}, f32[2560]{0:T(1024)}, u32[]{:S(2)}) copy-start(f32[2560]{0:T(1024)} %param.14) | copy-start | bytes 30724
  35.4 146.3 %all-gather.5.cloned.1.call-start = ((), (), s32[]{:S(2)}) async-start(), calls=%async_computation.6 | async-start | bytes 6963200 | tf_op jit(solution)/shard_map/all_gather | solution.py:245
  36.2 89.5 %collective-permute-start = (bf16[2560,1536]{1,0:T(8,128)(2,1)}, bf16[2560,1536]{1,0:T(8,128)(2,1)}, u32[]{:S(2)}, u32[]{:S(2)}) collective-permute-start(bf16[2560,1536]{1,0:T(8,128)(2,1)} %bitcast.54), channel_id=1, source_target_pairs={{8,1},{1,8},{10,3},{3,10},{12,5},{5,12},{14,7},{7,14},{24,17},{17,... | collective-permute-start | bytes 23592968 | tf_op jit(solution)/shard_map/ppermute | solution.py:240
  39.5 113.1 %collective-permute-start.1 = (bf16[384,2560]{1,0:T(8,128)(2,1)}, bf16[384,2560]{1,0:T(8,128)(2,1)}, u32[]{:S(2)}, u32[]{:S(2)}) collective-permute-start(bf16[384,2560]{1,0:T(8,128)(2,1)} %get-tuple-element.20), channel_id=1, source_target_pairs={{8,1},{1,8},{10,3},{3,10},{12,5},{5,12},{14,7},{7,14},{24,17},{17,... | collective-permute-start | bytes 5898248 | tf_op jit(solution)/shard_map/ppermute | solution.py:241
  130.8 26.3 %all-to-all-start.1 = ((bf16[8,128,512]{2,1,0:T(8,128)(2,1)}), bf16[8,128,512]{2,1,0:T(8,128)(2,1)S(1)}, u32[]{:S(2)}, u32[]{:S(2)}) async-start(bf16[8,128,512]{2,1,0:T(8,128)(2,1)} %shard_map.130), calls=%async_computation.1 | async-start | bytes 2097152 | tf_op jit(solution)/shard_map/all_to_all | solution.py:284
  134.4 27.5 %copy-start.8 = (s32[128,6]{0,1:T(8,128)S(1)}, s32[128,6]{0,1:T(8,128)}, u32[]{:S(2)}) copy-start(s32[128,6]{0,1:T(8,128)} %param.18) | copy-start | bytes 9220
  134.4 27.9 %copy-start = (f32[128,128]{1,0:T(8,128)S(1)}, f32[128,128]{1,0:T(8,128)}, u32[]{:S(2)}) copy-start(f32[128,128]{1,0:T(8,128)} %get-tuple-element.48.cosines) | copy-start | bytes 196612
  134.4 27.9 %copy-start.1 = (f32[128,128]{1,0:T(8,128)S(1)}, f32[128,128]{1,0:T(8,128)}, u32[]{:S(2)}) copy-start(f32[128,128]{1,0:T(8,128)} %get-tuple-element.49.sines) | copy-start | bytes 196612
  157.1 30.2 %collective-permute-start.2 = (bf16[384,2560]{1,0:T(8,128)(2,1)}, bf16[384,2560]{1,0:T(8,128)(2,1)}, u32[]{:S(2)}, u32[]{:S(2)}) collective-permute-start(bf16[384,2560]{1,0:T(8,128)(2,1)} %get-tuple-element.24), channel_id=1, source_target_pairs={{8,1},{1,8},{10,3},{3,10},{12,5},{5,12},{14,7},{7,14},{24,17},{17,... | collective-permute-start | bytes 5898248 | tf_op jit(solution)/shard_map/ppermute | solution.py:289
  166.4 19.3 %copy-start.6 = (f32[2560]{0:T(1024)S(1)}, f32[2560]{0:T(1024)}, u32[]{:S(2)}) copy-start(f32[2560]{0:T(1024)} %param.17) | copy-start | bytes 30724
  185.7 1.6 copy-start.3
  257.9 13.7 %collective-permute-start.3 = (bf16[1024,2560]{1,0:T(8,128)(2,1)}, bf16[1024,2560]{1,0:T(8,128)(2,1)}, u32[]{:S(2)}, u32[]{:S(2)}) collective-permute-start(bf16[1024,2560]{1,0:T(8,128)(2,1)} %bitcast.15.rows), channel_id=1, source_target_pairs={{0,8},{8,0},{1,9},{9,1},{2,10},{10,2},{3,11},{11,3},{4,12},{12,4},... | collective-permute-start | bytes 15728648 | tf_op jit(solution)/shard_map/ppermute | solution.py:302
  289.9 12.2 %collective-permute-start.4 = (bf16[1024,2560]{1,0:T(8,128)(2,1)}, bf16[1024,2560]{1,0:T(8,128)(2,1)}, u32[]{:S(2)}, u32[]{:S(2)}) collective-permute-start(bf16[1024,2560]{1,0:T(8,128)(2,1)} %shard_map.134), channel_id=1, source_target_pairs={{0,8},{8,0},{1,9},{9,1},{2,10},{10,2},{3,11},{11,3},{4,12},{12,4},... | collective-permute-start | bytes 15728648 | tf_op jit(solution)/shard_map/ppermute | solution.py:309
  309.8 5.8 %copy-start.7 = (f32[128,6]{0,1:T(8,128)S(1)}, f32[128,6]{0,1:T(8,128)}, u32[]{:S(2)}) copy-start(f32[128,6]{0,1:T(8,128)} %param.19) | copy-start | bytes 9220
  309.8 75.5 %all-to-all-start.3 = ((bf16[64,16,2560]{2,1,0:T(8,128)(2,1)}), bf16[64,16,2560]{2,1,0:T(8,128)(2,1)}, u32[]{:S(2)}, u32[]{:S(2)}) async-start(bf16[64,16,2560]{2,1,0:T(8,128)(2,1)} %bitcast.58), calls=%async_computation.3 | async-start | bytes 10485760 | tf_op jit(solution)/shard_map/all_to_all | solution.py:312
  385.3 4.2 %copy-start.4 = (f32[128,2560]{1,0:T(8,128)S(1)}, f32[128,2560]{1,0:T(8,128)}, u32[]{:S(2)}) copy-start(f32[128,2560]{1,0:T(8,128)} %copy-done.3) | copy-start | bytes 3932164
  390.5 15.3 %all-to-all-start.4 = ((bf16[8,16,2560]{2,1,0:T(8,128)(2,1)}), bf16[8,16,2560]{2,1,0:T(8,128)(2,1)S(1)}, u32[]{:S(2)}, u32[]{:S(2)}) async-start(bf16[8,16,2560]{2,1,0:T(8,128)(2,1)} %bitcast.19), calls=%async_computation.4 | async-start | bytes 1310720 | tf_op jit(solution)/shard_map/all_to_all | solution.py:321
Sparse Core Ops, SparseCore 0:
  35.5 76.9 all-gather.2
  115.0 66.6 all-gather.4

commit v4 on v3

--- a/solution.py
+++ b/solution.py
@@ -241,9 +241,15 @@
     other_first = lax.ppermute(sent_first, ALL, pairs)
     keep = lax.axis_index("x") % 2 == lax.axis_index("core")
 
-    full_qkv = lax.all_gather(qkv_rows, DP, axis=0, tiled=True)
-    full_out = lax.all_gather(out_rows, DP, axis=0, tiled=True)
-    full_qkv, other_up = lax.optimization_barrier((full_qkv, other_up))
+    out_halves = jnp.concatenate([out_rows[:, :half_out], out_rows[:, half_out:]], axis=0)
+    gathered = lax.all_gather(
+        jnp.concatenate([qkv_rows, out_halves], axis=1), DP, axis=0, tiled=True
+    )
+    gathered, other_up = lax.optimization_barrier((gathered, other_up))
+    full_qkv = gathered[:, : w_qkv.shape[1]]
+    out_parts = gathered[:, w_qkv.shape[1] :].reshape(-1, 2, out_rows.shape[0], half_out)
+    out_left = out_parts[:, 0].reshape(-1, half_out)
+    out_right = out_parts[:, 1].reshape(-1, half_out)
 
     my_place = lax.dynamic_slice_in_dim(placing, my_index * row_count, row_count)
     position = my_place - prompt_start
@@ -270,6 +276,7 @@
     weighted_hi = lax.reduce_precision(weighted, 8, 7)
     weighted_lo = (weighted - weighted_hi).astype(jnp.bfloat16)
     blend = jnp.concatenate([weighted_hi.astype(jnp.bfloat16), weighted_lo], axis=1)
+    blend = lax.optimization_barrier(blend.T)
 
     normed = rms_scaled(hidden_in, attn_gain)
     half_size = HD // 2
@@ -283,14 +290,20 @@
     kv_copies = keys_values(kv_projected, cosines, sines, cache_size)
     kv_group = lax.all_to_all(kv_copies, CACHE, 0, 0, tiled=True).reshape(group_rows, 2 * kv_width)
     projected = jnp.dot(normed, full_qkv[:, :query_width], preferred_element_type=jnp.float32)
-    kv_group, projected, other_first, sent_second = lax.optimization_barrier(
-        (kv_group, projected, other_first, w_down[0, down_half:])
+    kv_group, projected, out_left, out_right, other_first, sent_second = lax.optimization_barrier(
+        (kv_group, projected, out_left, out_right, other_first, w_down[0, down_half:])
     )
     other_second = lax.ppermute(sent_second, ALL, pairs)
     context = attention(
         projected, cosines, sines, kv_group, placing[None, :], prompt_start[:, None], my_place[:, None]
     )
-    attn_out = jnp.dot(context, full_out, preferred_element_type=jnp.float32)
+    attn_out = jnp.concatenate(
+        [
+            jnp.dot(context, part, preferred_element_type=jnp.float32)
+            for part in (out_left, out_right)
+        ],
+        axis=1,
+    )
     attended = (hidden_in.astype(jnp.float32) + attn_out).astype(jnp.bfloat16)
     moe_in = rms_scaled(attended, moe_gain)
 
@@ -312,9 +325,7 @@
     returned = lax.all_to_all(
         expert_out.reshape(CHIP_COUNT, MOST, model_width), CHIPS, 0, 0, tiled=True
     ).reshape(CHIP_COUNT * MOST, model_width)
-    blended = lax.dot_general(
-        blend, returned, (((0,), (0,)), ((), ())), preferred_element_type=jnp.float32
-    )
+    blended = jnp.dot(blend, returned, preferred_element_type=jnp.float32)
     mixture = blended[:row_count] + blended[row_count:]
     finished = (attended.astype(jnp.float32) + mixture).astype(jnp.bfloat16)
 

time: 416 us -> 416 us (level)
  local copies, waits for them, and re-layouts: 8.85 us -> 14.3 us
    ppermute x1, waiting for transfers between devices: 14.2 us -> 0.01 us  [per_device(): other_first = lax.ppermute(sent_first, ALL, pairs)]
    ppermute x1, waiting for transfers between devices: 0.01 us -> 12.8 us  [per_device(): other_second = lax.ppermute(sent_second, ALL, pairs)]
    slice x0 -> x4, local copies, waits for them, and re-layouts: none -> 6.07 us  [the longest x1 3.16 us: per_device(): out_right = out_parts[:, 1].reshape(-1, half_out)]
    all_gather x2 -> x1, waiting for transfers between devices: 15.3 us -> 15.8 us  [per_device(): lax.all_gather(jnp.concatenate([qkv_rows, out_halves], axis=1), DP, axis=...]
  transfers between devices with their start and end apart: 11 -> 10, of which waited for: 7 -> 7; matrix products, arithmetic and copies ran while one was open for 5% -> 6% of each run, Pallas kernels for 7% -> 7%
where the time goes in v4:
time: 416 us
  waiting for transfers between devices  209 us (50%)
  blocking collectives  68.4 us (16%)
  Pallas kernels  48.3 us (12%)
  starting transfers between devices  30.7 us (7%)
  matrix products  17.6 us (4%)
  between operations  14.5 us (3%)
  local copies, waits for them, and re-layouts  14.3 us (3%)
  other arithmetic  13.1 us (3%)
    ppermute x1, waiting for transfers between devices, per_device(): other_up = lax.ppermute(sent_up, ALL, pairs)  82.5 us
    all_to_all x1, waiting for transfers between devices, per_device(): lax.all_to_all(expert_out.reshape(CHIP_COUNT, MOST, model_width), CHIPS,...  68.9 us
    all_to_all x1, blocking collectives, per_device(): lax.all_to_all(outgoing.reshape(CHIP_COUNT, MOST, model_width), CHIPS, 0,...  68.4 us
    pallas_call x3, Pallas kernels, expert_half(): pl.pallas_call(expert_kernel, out_shape=jax.ShapeDtypeStruct(rows.shape,...  42 us
    all_gather x1, waiting for transfers between devices, per_device(): lax.all_gather(jnp.concatenate([qkv_rows, out_halves], axis=1), DP, axis=...  15.8 us
    ppermute x1, waiting for transfers between devices, per_device(): other_second = lax.ppermute(sent_second, ALL, pairs)  12.8 us
    all_to_all x1, waiting for transfers between devices, spread(): lax.all_to_all(jnp.broadcast_to(shard[None], (count,) + shard.shape), axe...  12.8 us
    all_to_all x1, waiting for transfers between devices, per_device(): lax.all_to_all(finished.reshape(cache_size, deal_rows, model_width), CACH...  10.2 us
  transfers between devices with their start and end apart: 10, of which 7 were waited for; matrix products, arithmetic and copies ran while one was open for 6% of the time, Pallas kernels for 7%

profile of v4, /device:TPU:1, one launch (start us, length us, event | category | flops | bytes accessed | tf_op | source)
XLA Modules:
  0.0 415.5 jit_solution(2226400570203677148)
XLA Ops:
  10.1 5.9 %all-to-all-start = ((bf16[8,20,3072]{2,1,0:T(8,128)(2,1)}), bf16[8,20,3072]{2,1,0:T(8,128)(2,1)S(1)}, u32[]{:S(2)}, u32[]{:S(2)}) async-start(bf16[8,20,3072]{2,1,0:T(8,128)(2,1)} %broadcast_in_dim.38), calls=%async_computation | async-start | bytes 2359296 | tf_op jit(solution)/shard_map/all_to_all | solution.py:106
  16.0 4.4 %slice_bitcast_fusion = (bf16[384,2560]{1,0:T(8,128)(2,1)}, bf16[384,2560]{1,0:T(8,128)(2,1)}) fusion(bf16[1,768,2560]{2,1,0:T(8,128)(2,1)} %param.21), kind=kLoop, calls=%fused_computation.10 | loop fusion | bytes 7864320 | tf_op jit(solution)/shard_map/squeeze | solution.py:294
  20.4 12.8 %all-to-all-done = bf16[8,20,3072]{2,1,0:T(8,128)(2,1)S(1)} async-done(((bf16[8,20,3072]{2,1,0:T(8,128)(2,1)}), bf16[8,20,3072]{2,1,0:T(8,128)(2,1)S(1)}, u32[]{:S(2)}, u32[]{:S(2)}) %all-to-all-start) | async-done | bytes 983072 | tf_op jit(solution)/shard_map/all_to_all | solution.py:106
  34.9 3.2 collective-permute-start
  42.0 82.5 %collective-permute-done.other_up = bf16[2560,1536]{1,0:T(8,128)(2,1)} collective-permute-done((bf16[2560,1536]{1,0:T(8,128)(2,1)}, bf16[2560,1536]{1,0:T(8,128)(2,1)}, u32[]{:S(2)}, u32[]{:S(2)}) %collective-permute-start) | collective-permute-done | bytes 7864352 | tf_op jit(solution)/shard_map/ppermute | solution.py:240
  124.4 15.8 %all-gather.2.cloned.1.call-done = bf16[2560,3072]{1,0:T(8,128)(2,1)} async-done(((bf16[160,3072]{1,0:T(8,128)(2,1)}), bf16[2560,3072]{1,0:T(8,128)(2,1)}) %all-gather.2.cloned.1.call-update) | async-done | bytes 15728656 | tf_op jit(solution)/shard_map/all_gather | solution.py:245
  140.2 3.0 fusion.2.projected
  145.4 4.0 all-to-all-start.1
  149.4 4.0 fusion.projected
  156.3 3.2 fusion.24
  159.5 5.8 %all-to-all-done.1 = bf16[8,128,512]{2,1,0:T(8,128)(2,1)S(1)} async-done(((bf16[8,128,512]{2,1,0:T(8,128)(2,1)}), bf16[8,128,512]{2,1,0:T(8,128)(2,1)S(1)}, u32[]{:S(2)}, u32[]{:S(2)}) %all-to-all-start.1) | async-done | bytes 1048608 | tf_op jit(solution)/shard_map/all_to_all | solution.py:291
  165.3 3.1 collective-permute-start.2
  169.2 4.1 shard_map.131
  178.7 12.8 %collective-permute-done.2.other_second = bf16[384,2560]{1,0:T(8,128)(2,1)} collective-permute-done((bf16[384,2560]{1,0:T(8,128)(2,1)}, bf16[384,2560]{1,0:T(8,128)(2,1)}, u32[]{:S(2)}, u32[]{:S(2)}) %collective-permute-start.2) | collective-permute-done | bytes 1966112 | tf_op jit(solution)/shard_map/ppermute | solution.py:296
  191.5 68.4 %all_to_all.25 = bf16[64,16,2560]{2,1,0:T(8,128)(2,1)} all-to-all(bf16[64,16,2560]{2,1,0:T(8,128)(2,1)S(1)} %bitcast.58), channel_id=1, replica_groups=mesh['yh'=2,'z'=4,'core'=2,'yl'=2,'x'=4] {'yh','z','yl','x'}, dimensions={0} | all-to-all | bytes 10485760 | tf_op jit(solution)/shard_map/all_to_all | solution.py:312
  261.5 11.9 %shard_map.132.rest_0_ = bf16[1024,2560]{1,0:T(8,128)(2,1)} custom-call(s32[1]{0:T(128)} %bitcast.17.keep, bf16[1024,2560]{1,0:T(8,128)(2,1)} %bitcast.19.rows, bf16[2560,1536]{1,0:T(8,128)(2,1)} %bitcast.63, bf16[2560,1536]{1,0:T(8,128)(2,1)} %collective-permute-done.other_up, bf16[768,2560]{1,0:T(8,128)(2,1)} %bitcast.59, ...), custom_call_target="tpu_custom_call" | custom-call | flops 6039797760 | bytes 17039360 | tf_op jit(solution)/shard_map/pallas_call | solution.py:176
  273.5 18.3 %shard_map.134 = bf16[1024,2560]{1,0:T(8,128)(2,1)} custom-call(s32[1]{0:T(128)} %bitcast.17.keep, bf16[1024,2560]{1,0:T(8,128)(2,1)} %collective-permute-done.3.rows, bf16[2560,1536]{1,0:T(8,128)(2,1)} %bitcast.64, bf16[2560,1536]{1,0:T(8,128)(2,1)} %collective-permute-done.other_up, bf16[768,2560]{1,0:T(8,128)(2,1)} %bitcast.60, ...), custom_call_target="tpu_custom_call" | custom-call | flops 12079595520 | bytes 22282240 | tf_op jit(solution)/shard_map/pallas_call | solution.py:176
  292.1 11.8 %shard_map.133 = bf16[1024,2560]{1,0:T(8,128)(2,1)} custom-call(s32[1]{0:T(128)} %bitcast.17.keep, bf16[1024,2560]{1,0:T(8,128)(2,1)} %bitcast.19.rows, bf16[2560,1536]{1,0:T(8,128)(2,1)} %bitcast.65, bf16[2560,1536]{1,0:T(8,128)(2,1)} %collective-permute-done.other_up, bf16[768,2560]{1,0:T(8,128)(2,1)} %bitcast.61, ...), custom_call_target="tpu_custom_call", output_to_operand_aliasing={{}: (7, {})} | custom-call | flops 6039797760 | bytes 17039360 | tf_op jit(solution)/shard_map/pallas_call | solution.py:176
  303.9 7.7 %add_convert_fusion = bf16[1024,2560]{1,0:T(8,128)(2,1)} fusion(bf16[1024,2560]{1,0:T(8,128)(2,1)} %collective-permute-done.4, bf16[1024,2560]{1,0:T(8,128)(2,1)} %shard_map.133), kind=kLoop, calls=%fused_computation | loop fusion | flops 10485760 | bytes 15728640 | tf_op jit(solution)/shard_map/convert_element_type | solution.py:324
  311.6 5.8 %all-to-all-start.3 = ((bf16[64,16,2560]{2,1,0:T(8,128)(2,1)}), bf16[64,16,2560]{2,1,0:T(8,128)(2,1)}, u32[]{:S(2)}, u32[]{:S(2)}) async-start(bf16[64,16,2560]{2,1,0:T(8,128)(2,1)} %bitcast.67), calls=%async_computation.3 | async-start | bytes 10485760 | tf_op jit(solution)/shard_map/all_to_all | solution.py:325
  317.8 68.9 %all-to-all-done.3 = bf16[64,16,2560]{2,1,0:T(8,128)(2,1)} async-done(((bf16[64,16,2560]{2,1,0:T(8,128)(2,1)}), bf16[64,16,2560]{2,1,0:T(8,128)(2,1)}, u32[]{:S(2)}, u32[]{:S(2)}) %all-to-all-start.3) | async-done | bytes 5242912 | tf_op jit(solution)/shard_map/all_to_all | solution.py:325
  386.7 4.1 fusion.31
  391.8 4.3 %all-to-all-start.4 = ((bf16[8,16,2560]{2,1,0:T(8,128)(2,1)}), bf16[8,16,2560]{2,1,0:T(8,128)(2,1)S(1)}, u32[]{:S(2)}, u32[]{:S(2)}) async-start(bf16[8,16,2560]{2,1,0:T(8,128)(2,1)} %bitcast.23), calls=%async_computation.4 | async-start | bytes 1310720 | tf_op jit(solution)/shard_map/all_to_all | solution.py:332
  397.3 10.2 %all-to-all-done.4 = bf16[8,16,2560]{2,1,0:T(8,128)(2,1)S(1)} async-done(((bf16[8,16,2560]{2,1,0:T(8,128)(2,1)}), bf16[8,16,2560]{2,1,0:T(8,128)(2,1)S(1)}, u32[]{:S(2)}, u32[]{:S(2)}) %all-to-all-start.4) | async-done | bytes 655392 | tf_op jit(solution)/shard_map/all_to_all | solution.py:332
  (75 shorter events, 25.1 us)
Async XLA Ops:
  10.1 23.1 %all-to-all-start = ((bf16[8,20,3072]{2,1,0:T(8,128)(2,1)}), bf16[8,20,3072]{2,1,0:T(8,128)(2,1)S(1)}, u32[]{:S(2)}, u32[]{:S(2)}) async-start(bf16[8,20,3072]{2,1,0:T(8,128)(2,1)} %broadcast_in_dim.38), calls=%async_computation | async-start | bytes 2359296 | tf_op jit(solution)/shard_map/all_to_all | solution.py:106
  15.9 124.3 %all-gather.2.cloned.1.call-start = ((), (), s32[]{:S(2)}) async-start(), calls=%async_computation.5 | async-start | bytes 16711680 | tf_op jit(solution)/shard_map/all_gather | solution.py:245
  33.7 4.5 %copy-start.4 = (bf16[128,2560]{1,0:T(8,128)(2,1)S(1)}, bf16[128,2560]{1,0:T(8,128)(2,1)}, u32[]{:S(2)}) copy-start(bf16[128,2560]{1,0:T(8,128)(2,1)} %param.11) | copy-start | bytes 1966084
  33.8 4.6 %copy-start.2 = (s32[1024]{0:T(1024)S(1)}, s32[1024]{0:T(1024)}, u32[]{:S(2)}) copy-start(s32[1024]{0:T(1024)} %param.12) | copy-start | bytes 12292
  33.8 4.6 %copy-start.8 = (s32[128]{0:T(128)S(1)}, s32[128]{0:T(128)}, u32[]{:S(2)}) copy-start(s32[128]{0:T(128)} %param.13) | copy-start | bytes 1540
  33.8 106.4 %copy-start.9 = (f32[2560]{0:T(1024)S(1)}, f32[2560]{0:T(1024)}, u32[]{:S(2)}) copy-start(f32[2560]{0:T(1024)} %param.14) | copy-start | bytes 30724
  34.9 89.5 %collective-permute-start = (bf16[2560,1536]{1,0:T(8,128)(2,1)}, bf16[2560,1536]{1,0:T(8,128)(2,1)}, u32[]{:S(2)}, u32[]{:S(2)}) collective-permute-start(bf16[2560,1536]{1,0:T(8,128)(2,1)} %bitcast.62), channel_id=1, source_target_pairs={{8,1},{1,8},{10,3},{3,10},{12,5},{5,12},{14,7},{7,14},{24,17},{17,... | collective-permute-start | bytes 23592968 | tf_op jit(solution)/shard_map/ppermute | solution.py:240
  38.8 120.7 %collective-permute-start.1 = (bf16[384,2560]{1,0:T(8,128)(2,1)}, bf16[384,2560]{1,0:T(8,128)(2,1)}, u32[]{:S(2)}, u32[]{:S(2)}) collective-permute-start(bf16[384,2560]{1,0:T(8,128)(2,1)} %get-tuple-element.23), channel_id=1, source_target_pairs={{8,1},{1,8},{10,3},{3,10},{12,5},{5,12},{14,7},{7,14},{24,17},{17,... | collective-permute-start | bytes 5898248 | tf_op jit(solution)/shard_map/ppermute | solution.py:241
  145.4 19.9 %all-to-all-start.1 = ((bf16[8,128,512]{2,1,0:T(8,128)(2,1)}), bf16[8,128,512]{2,1,0:T(8,128)(2,1)S(1)}, u32[]{:S(2)}, u32[]{:S(2)}) async-start(bf16[8,128,512]{2,1,0:T(8,128)(2,1)} %shard_map.130), calls=%async_computation.1 | async-start | bytes 2097152 | tf_op jit(solution)/shard_map/all_to_all | solution.py:291
  153.4 2.9 slice-start
  156.3 12.1 %copy-start.7 = (s32[128,6]{0,1:T(8,128)S(1)}, s32[128,6]{0,1:T(8,128)}, u32[]{:S(2)}) copy-start(s32[128,6]{0,1:T(8,128)} %param.18) | copy-start | bytes 9220
  156.3 12.8 %copy-start = (f32[128,128]{1,0:T(8,128)S(1)}, f32[128,128]{1,0:T(8,128)}, u32[]{:S(2)}) copy-start(f32[128,128]{1,0:T(8,128)} %get-tuple-element.56.cosines) | copy-start | bytes 196612
  156.3 12.8 %copy-start.1 = (f32[128,128]{1,0:T(8,128)S(1)}, f32[128,128]{1,0:T(8,128)}, u32[]{:S(2)}) copy-start(f32[128,128]{1,0:T(8,128)} %get-tuple-element.57.sines) | copy-start | bytes 196612
  165.3 26.3 %collective-permute-start.2 = (bf16[384,2560]{1,0:T(8,128)(2,1)}, bf16[384,2560]{1,0:T(8,128)(2,1)}, u32[]{:S(2)}, u32[]{:S(2)}) collective-permute-start(bf16[384,2560]{1,0:T(8,128)(2,1)} %get-tuple-element.28), channel_id=1, source_target_pairs={{8,1},{1,8},{10,3},{3,10},{12,5},{5,12},{14,7},{7,14},{24,17},{17,... | collective-permute-start | bytes 5898248 | tf_op jit(solution)/shard_map/ppermute | solution.py:296
  173.3 2.9 copy-start.3
  176.2 0.9 copy-start.5
  259.9 13.6 %collective-permute-start.3 = (bf16[1024,2560]{1,0:T(8,128)(2,1)}, bf16[1024,2560]{1,0:T(8,128)(2,1)}, u32[]{:S(2)}, u32[]{:S(2)}) collective-permute-start(bf16[1024,2560]{1,0:T(8,128)(2,1)} %bitcast.19.rows), channel_id=1, source_target_pairs={{0,8},{8,0},{1,9},{9,1},{2,10},{10,2},{3,11},{11,3},{4,12},{12,4},... | collective-permute-start | bytes 15728648 | tf_op jit(solution)/shard_map/ppermute | solution.py:315
  291.8 12.1 %collective-permute-start.4 = (bf16[1024,2560]{1,0:T(8,128)(2,1)}, bf16[1024,2560]{1,0:T(8,128)(2,1)}, u32[]{:S(2)}, u32[]{:S(2)}) collective-permute-start(bf16[1024,2560]{1,0:T(8,128)(2,1)} %shard_map.134), channel_id=1, source_target_pairs={{0,8},{8,0},{1,9},{9,1},{2,10},{10,2},{3,11},{11,3},{4,12},{12,4},... | collective-permute-start | bytes 15728648 | tf_op jit(solution)/shard_map/ppermute | solution.py:322
  311.6 5.8 %copy-start.6 = (f32[128,6]{0,1:T(8,128)S(1)}, f32[128,6]{0,1:T(8,128)}, u32[]{:S(2)}) copy-start(f32[128,6]{0,1:T(8,128)} %param.19) | copy-start | bytes 9220
  311.6 75.0 %all-to-all-start.3 = ((bf16[64,16,2560]{2,1,0:T(8,128)(2,1)}), bf16[64,16,2560]{2,1,0:T(8,128)(2,1)}, u32[]{:S(2)}, u32[]{:S(2)}) async-start(bf16[64,16,2560]{2,1,0:T(8,128)(2,1)} %bitcast.67), calls=%async_computation.3 | async-start | bytes 10485760 | tf_op jit(solution)/shard_map/all_to_all | solution.py:325
  391.8 15.7 %all-to-all-start.4 = ((bf16[8,16,2560]{2,1,0:T(8,128)(2,1)}), bf16[8,16,2560]{2,1,0:T(8,128)(2,1)S(1)}, u32[]{:S(2)}, u32[]{:S(2)}) async-start(bf16[8,16,2560]{2,1,0:T(8,128)(2,1)} %bitcast.23), calls=%async_computation.4 | async-start | bytes 1310720 | tf_op jit(solution)/shard_map/all_to_all | solution.py:332
Sparse Core Ops, SparseCore 0:
  35.1 105.0 all-gather.1

commit v5 on v4

--- a/solution.py
+++ b/solution.py
@@ -123,10 +123,10 @@
         source = own_up if mine else other_up
         return pltpu.make_async_copy(source.at[part], up.at[part], up_sems.at[i])
 
-    down_half = down.shape[0] // 2
+    first_rows = other_first.shape[0]
 
     def down_copy(i, mine):
-        part = pl.ds(i * down_half, down_half)
+        part = (pl.ds(0, first_rows), pl.ds(first_rows, down.shape[0] - first_rows))[i]
         source = own_down.at[part] if mine else (other_first, other_second)[i]
         return pltpu.make_async_copy(source, down.at[part], down_sems.at[i])
 
@@ -233,9 +233,9 @@
     out_rows = jnp.concatenate([halves[:, 0], halves[:, 1]], axis=2).reshape(-1, w_out.shape[1])
 
     pairs = swap_pairs()
-    down_half = w_down.shape[1] // 2
+    first_rows = w_down.shape[1] * 3 // 4
     sent_up, sent_first, qkv_rows, out_rows = lax.optimization_barrier(
-        (w_gate_up[0], w_down[0, :down_half], qkv_rows, out_rows)
+        (w_gate_up[0], w_down[0, :first_rows], qkv_rows, out_rows)
     )
     other_up = lax.ppermute(sent_up, ALL, pairs)
     other_first = lax.ppermute(sent_first, ALL, pairs)
@@ -291,7 +291,7 @@
     kv_group = lax.all_to_all(kv_copies, CACHE, 0, 0, tiled=True).reshape(group_rows, 2 * kv_width)
     projected = jnp.dot(normed, full_qkv[:, :query_width], preferred_element_type=jnp.float32)
     kv_group, projected, out_left, out_right, other_first, sent_second = lax.optimization_barrier(
-        (kv_group, projected, out_left, out_right, other_first, w_down[0, down_half:])
+        (kv_group, projected, out_left, out_right, other_first, w_down[0, first_rows:])
     )
     other_second = lax.ppermute(sent_second, ALL, pairs)
     context = attention(

time: 416 us -> 416 us (level)
  waiting for transfers between devices: 209 us -> 198 us
  blocking collectives: 68.4 us -> 73.8 us
    ppermute x1, waiting for transfers between devices: 12.8 us -> 2.27 us  [per_device(): other_second = lax.ppermute(sent_second, ALL, pairs)]
    all_to_all x1, blocking collectives: 68.4 us -> 73.8 us  [per_device(): lax.all_to_all(outgoing.reshape(CHIP_COUNT, MOST, model_width), CHIPS, 0,...]
  transfers between devices with their start and end apart: 10 -> 10, of which waited for: 7 -> 8; matrix products, arithmetic and copies ran while one was open for 6% -> 6% of each run, Pallas kernels for 7% -> 7%
where the time goes in v5:
time: 416 us; the launch traced here: 415 us
  waiting for transfers between devices  198 us (48%)
  blocking collectives  73.8 us (18%)
  Pallas kernels  48.5 us (12%)
  starting transfers between devices  33.7 us (8%)
  matrix products  17.4 us (4%)
  local copies, waits for them, and re-layouts  16 us (4%)
  between operations  14.5 us (3%)
  other arithmetic  13.1 us (3%)
    ppermute x1, waiting for transfers between devices, per_device(): other_up = lax.ppermute(sent_up, ALL, pairs)  79.5 us
    all_to_all x1, blocking collectives, per_device(): lax.all_to_all(outgoing.reshape(CHIP_COUNT, MOST, model_width), CHIPS, 0,...  73.8 us
    all_to_all x1, waiting for transfers between devices, per_device(): lax.all_to_all(expert_out.reshape(CHIP_COUNT, MOST, model_width), CHIPS,...  70 us
    pallas_call x3, Pallas kernels, expert_half(): pl.pallas_call(expert_kernel, out_shape=jax.ShapeDtypeStruct(rows.shape,...  42.2 us
    all_gather x1, waiting for transfers between devices, per_device(): lax.all_gather(jnp.concatenate([qkv_rows, out_halves], axis=1), DP, axis=...  15.8 us
    all_to_all x1, waiting for transfers between devices, spread(): lax.all_to_all(jnp.broadcast_to(shard[None], (count,) + shard.shape), axe...  13.5 us
    all_to_all x1, waiting for transfers between devices, per_device(): lax.all_to_all(finished.reshape(cache_size, deal_rows, model_width), CACH...  10.5 us
  transfers between devices with their start and end apart: 10, of which 8 were waited for; matrix products, arithmetic and copies ran while one was open for 6% of the time, Pallas kernels for 7%

profile of v5, /device:TPU:1, one launch (start us, length us, event | category | flops | bytes accessed | tf_op | source)
XLA Modules:
  0.0 415.3 jit_solution(1879667041979305080)
XLA Ops:
  10.1 5.9 %all-to-all-start = ((bf16[8,20,3072]{2,1,0:T(8,128)(2,1)}), bf16[8,20,3072]{2,1,0:T(8,128)(2,1)S(1)}, u32[]{:S(2)}, u32[]{:S(2)}) async-start(bf16[8,20,3072]{2,1,0:T(8,128)(2,1)} %broadcast_in_dim.38), calls=%async_computation | async-start | bytes 2359296 | tf_op jit(solution)/shard_map/all_to_all | solution.py:106
  16.0 3.7 slice_bitcast_fusion
  19.6 13.5 %all-to-all-done = bf16[8,20,3072]{2,1,0:T(8,128)(2,1)S(1)} async-done(((bf16[8,20,3072]{2,1,0:T(8,128)(2,1)}), bf16[8,20,3072]{2,1,0:T(8,128)(2,1)S(1)}, u32[]{:S(2)}, u32[]{:S(2)}) %all-to-all-start) | async-done | bytes 983072 | tf_op jit(solution)/shard_map/all_to_all | solution.py:106
  35.0 3.2 collective-permute-start
  45.0 79.5 %collective-permute-done.other_up = bf16[2560,1536]{1,0:T(8,128)(2,1)} collective-permute-done((bf16[2560,1536]{1,0:T(8,128)(2,1)}, bf16[2560,1536]{1,0:T(8,128)(2,1)}, u32[]{:S(2)}, u32[]{:S(2)}) %collective-permute-start) | collective-permute-done | bytes 7864352 | tf_op jit(solution)/shard_map/ppermute | solution.py:240
  124.5 15.8 %all-gather.2.cloned.1.call-done = bf16[2560,3072]{1,0:T(8,128)(2,1)} async-done(((bf16[160,3072]{1,0:T(8,128)(2,1)}), bf16[2560,3072]{1,0:T(8,128)(2,1)}) %all-gather.2.cloned.1.call-update) | async-done | bytes 15728656 | tf_op jit(solution)/shard_map/all_gather | solution.py:245
  140.2 3.0 fusion.2.projected
  145.4 4.0 all-to-all-start.1
  149.4 3.9 fusion.projected
  153.4 2.9 slice-done
  156.2 3.2 fusion.24
  160.1 6.0 %all-to-all-done.1 = bf16[8,128,512]{2,1,0:T(8,128)(2,1)S(1)} async-done(((bf16[8,128,512]{2,1,0:T(8,128)(2,1)}), bf16[8,128,512]{2,1,0:T(8,128)(2,1)S(1)}, u32[]{:S(2)}, u32[]{:S(2)}) %all-to-all-start.1) | async-done | bytes 1048608 | tf_op jit(solution)/shard_map/all_to_all | solution.py:291
  166.1 4.5 %collective-permute-start.2 = (bf16[192,2560]{1,0:T(8,128)(2,1)}, bf16[192,2560]{1,0:T(8,128)(2,1)S(1)}, u32[]{:S(2)}, u32[]{:S(2)}) collective-permute-start(bf16[192,2560]{1,0:T(8,128)(2,1)} %slice_bitcast_fusion.1), channel_id=1, source_target_pairs={{8,1},{1,8},{10,3},{3,10},{12,5},{5,12},{14,7},{7,14},{24,17},{17,... | collective-permute-start | bytes 2949128 | tf_op jit(solution)/shard_map/ppermute | solution.py:296
  170.7 4.1 shard_map.131
  182.6 73.8 %all_to_all.25 = bf16[64,16,2560]{2,1,0:T(8,128)(2,1)} all-to-all(bf16[64,16,2560]{2,1,0:T(8,128)(2,1)S(1)} %bitcast.58), channel_id=1, replica_groups=mesh['yh'=2,'z'=4,'core'=2,'yl'=2,'x'=4] {'yh','z','yl','x'}, dimensions={0} | all-to-all | bytes 10485760 | tf_op jit(solution)/shard_map/all_to_all | solution.py:312
  258.2 11.9 %shard_map.132.rest_0_ = bf16[1024,2560]{1,0:T(8,128)(2,1)} custom-call(s32[1]{0:T(128)} %bitcast.17.keep, bf16[1024,2560]{1,0:T(8,128)(2,1)} %bitcast.19.rows, bf16[2560,1536]{1,0:T(8,128)(2,1)} %bitcast.63, bf16[2560,1536]{1,0:T(8,128)(2,1)} %collective-permute-done.other_up, bf16[768,2560]{1,0:T(8,128)(2,1)} %bitcast.59, ...), custom_call_target="tpu_custom_call" | custom-call | flops 6039797760 | bytes 17039360 | tf_op jit(solution)/shard_map/pallas_call | solution.py:176
  270.2 18.4 %shard_map.134 = bf16[1024,2560]{1,0:T(8,128)(2,1)} custom-call(s32[1]{0:T(128)} %bitcast.17.keep, bf16[1024,2560]{1,0:T(8,128)(2,1)} %collective-permute-done.3.rows, bf16[2560,1536]{1,0:T(8,128)(2,1)} %bitcast.64, bf16[2560,1536]{1,0:T(8,128)(2,1)} %collective-permute-done.other_up, bf16[768,2560]{1,0:T(8,128)(2,1)} %bitcast.60, ...), custom_call_target="tpu_custom_call" | custom-call | flops 12079595520 | bytes 22282240 | tf_op jit(solution)/shard_map/pallas_call | solution.py:176
  288.9 11.9 %shard_map.133 = bf16[1024,2560]{1,0:T(8,128)(2,1)} custom-call(s32[1]{0:T(128)} %bitcast.17.keep, bf16[1024,2560]{1,0:T(8,128)(2,1)} %bitcast.19.rows, bf16[2560,1536]{1,0:T(8,128)(2,1)} %bitcast.65, bf16[2560,1536]{1,0:T(8,128)(2,1)} %collective-permute-done.other_up, bf16[768,2560]{1,0:T(8,128)(2,1)} %bitcast.61, ...), custom_call_target="tpu_custom_call", output_to_operand_aliasing={{}: (7, {})} | custom-call | flops 6039797760 | bytes 17039360 | tf_op jit(solution)/shard_map/pallas_call | solution.py:176
  300.8 7.7 %add_convert_fusion = bf16[1024,2560]{1,0:T(8,128)(2,1)} fusion(bf16[1024,2560]{1,0:T(8,128)(2,1)} %collective-permute-done.4, bf16[1024,2560]{1,0:T(8,128)(2,1)} %shard_map.133), kind=kLoop, calls=%fused_computation | loop fusion | flops 10485760 | bytes 15728640 | tf_op jit(solution)/shard_map/convert_element_type | solution.py:324
  308.5 5.8 %all-to-all-start.3 = ((bf16[64,16,2560]{2,1,0:T(8,128)(2,1)}), bf16[64,16,2560]{2,1,0:T(8,128)(2,1)}, u32[]{:S(2)}, u32[]{:S(2)}) async-start(bf16[64,16,2560]{2,1,0:T(8,128)(2,1)} %bitcast.67), calls=%async_computation.3 | async-start | bytes 10485760 | tf_op jit(solution)/shard_map/all_to_all | solution.py:325
  314.7 70.0 %all-to-all-done.3 = bf16[64,16,2560]{2,1,0:T(8,128)(2,1)} async-done(((bf16[64,16,2560]{2,1,0:T(8,128)(2,1)}), bf16[64,16,2560]{2,1,0:T(8,128)(2,1)}, u32[]{:S(2)}, u32[]{:S(2)}) %all-to-all-start.3) | async-done | bytes 5242912 | tf_op jit(solution)/shard_map/all_to_all | solution.py:325
  384.7 4.1 fusion.31
  389.8 5.9 %all-to-all-start.4 = ((bf16[8,16,2560]{2,1,0:T(8,128)(2,1)}), bf16[8,16,2560]{2,1,0:T(8,128)(2,1)S(1)}, u32[]{:S(2)}, u32[]{:S(2)}) async-start(bf16[8,16,2560]{2,1,0:T(8,128)(2,1)} %bitcast.23), calls=%async_computation.4 | async-start | bytes 1310720 | tf_op jit(solution)/shard_map/all_to_all | solution.py:332
  396.8 10.5 %all-to-all-done.4 = bf16[8,16,2560]{2,1,0:T(8,128)(2,1)S(1)} async-done(((bf16[8,16,2560]{2,1,0:T(8,128)(2,1)}), bf16[8,16,2560]{2,1,0:T(8,128)(2,1)S(1)}, u32[]{:S(2)}, u32[]{:S(2)}) %all-to-all-start.4) | async-done | bytes 655392 | tf_op jit(solution)/shard_map/all_to_all | solution.py:332
  (80 shorter events, 27.7 us)
Async XLA Ops:
  10.1 23.1 %all-to-all-start = ((bf16[8,20,3072]{2,1,0:T(8,128)(2,1)}), bf16[8,20,3072]{2,1,0:T(8,128)(2,1)S(1)}, u32[]{:S(2)}, u32[]{:S(2)}) async-start(bf16[8,20,3072]{2,1,0:T(8,128)(2,1)} %broadcast_in_dim.38), calls=%async_computation | async-start | bytes 2359296 | tf_op jit(solution)/shard_map/all_to_all | solution.py:106
  15.9 124.3 %all-gather.2.cloned.1.call-start = ((), (), s32[]{:S(2)}) async-start(), calls=%async_computation.5 | async-start | bytes 16711680 | tf_op jit(solution)/shard_map/all_gather | solution.py:245
  33.6 4.6 %copy-start.9 = (s32[128,6]{0,1:T(8,128)S(1)}, s32[128,6]{0,1:T(8,128)}, u32[]{:S(2)}) copy-start(s32[128,6]{0,1:T(8,128)} %param.18) | copy-start | bytes 9220
  33.6 4.7 %copy-start.2 = (s32[1024]{0:T(1024)S(1)}, s32[1024]{0:T(1024)}, u32[]{:S(2)}) copy-start(s32[1024]{0:T(1024)} %param.12) | copy-start | bytes 12292
  33.6 4.7 %copy-start.10 = (s32[128]{0:T(128)S(1)}, s32[128]{0:T(128)}, u32[]{:S(2)}) copy-start(s32[128]{0:T(128)} %param.13) | copy-start | bytes 1540
  33.7 8.8 %copy-start.5 = (bf16[128,2560]{1,0:T(8,128)(2,1)S(1)}, bf16[128,2560]{1,0:T(8,128)(2,1)}, u32[]{:S(2)}) copy-start(bf16[128,2560]{1,0:T(8,128)(2,1)} %param.11) | copy-start | bytes 1966084
  33.9 106.4 %copy-start.11 = (f32[2560]{0:T(1024)S(1)}, f32[2560]{0:T(1024)}, u32[]{:S(2)}) copy-start(f32[2560]{0:T(1024)} %param.14) | copy-start | bytes 30724
  35.0 89.5 %collective-permute-start = (bf16[2560,1536]{1,0:T(8,128)(2,1)}, bf16[2560,1536]{1,0:T(8,128)(2,1)}, u32[]{:S(2)}, u32[]{:S(2)}) collective-permute-start(bf16[2560,1536]{1,0:T(8,128)(2,1)} %bitcast.62), channel_id=1, source_target_pairs={{8,1},{1,8},{10,3},{3,10},{12,5},{5,12},{14,7},{7,14},{24,17},{17,... | collective-permute-start | bytes 23592968 | tf_op jit(solution)/shard_map/ppermute | solution.py:240
  38.7 121.4 %collective-permute-start.1 = (bf16[576,2560]{1,0:T(8,128)(2,1)}, bf16[576,2560]{1,0:T(8,128)(2,1)}, u32[]{:S(2)}, u32[]{:S(2)}) collective-permute-start(bf16[576,2560]{1,0:T(8,128)(2,1)} %slice_bitcast_fusion), channel_id=1, source_target_pairs={{8,1},{1,8},{10,3},{3,10},{12,5},{5,12},{14,7},{7,14},{24,17},{17,... | collective-permute-start | bytes 8847368 | tf_op jit(solution)/shard_map/ppermute | solution.py:241
  145.4 20.7 %all-to-all-start.1 = ((bf16[8,128,512]{2,1,0:T(8,128)(2,1)}), bf16[8,128,512]{2,1,0:T(8,128)(2,1)S(1)}, u32[]{:S(2)}, u32[]{:S(2)}) async-start(bf16[8,128,512]{2,1,0:T(8,128)(2,1)} %shard_map.130), calls=%async_computation.1 | async-start | bytes 2097152 | tf_op jit(solution)/shard_map/all_to_all | solution.py:291
  153.4 2.9 slice-start
  156.2 14.4 %copy-start = (f32[128,128]{1,0:T(8,128)S(1)}, f32[128,128]{1,0:T(8,128)}, u32[]{:S(2)}) copy-start(f32[128,128]{1,0:T(8,128)} %get-tuple-element.54.cosines) | copy-start | bytes 196612
  156.2 14.4 %copy-start.1 = (f32[128,128]{1,0:T(8,128)S(1)}, f32[128,128]{1,0:T(8,128)}, u32[]{:S(2)}) copy-start(f32[128,128]{1,0:T(8,128)} %get-tuple-element.55.sines) | copy-start | bytes 196612
  166.1 16.5 %collective-permute-start.2 = (bf16[192,2560]{1,0:T(8,128)(2,1)}, bf16[192,2560]{1,0:T(8,128)(2,1)S(1)}, u32[]{:S(2)}, u32[]{:S(2)}) collective-permute-start(bf16[192,2560]{1,0:T(8,128)(2,1)} %slice_bitcast_fusion.1), channel_id=1, source_target_pairs={{8,1},{1,8},{10,3},{3,10},{12,5},{5,12},{14,7},{7,14},{24,17},{17,... | collective-permute-start | bytes 2949128 | tf_op jit(solution)/shard_map/ppermute | solution.py:296
  170.7 6.7 %copy-start.3 = (bf16[16,1,80,1280]{3,2,1,0:T(8,128)(2,1)S(1)}, bf16[16,1,80,1280]{3,2,1,0:T(8,128)(2,1)}, u32[]{:S(2)}) copy-start(bf16[16,1,80,1280]{3,2,1,0:T(8,128)(2,1)} %get-tuple-element.38) | copy-start | bytes 9830404
  177.3 1.1 copy-start.6
  177.4 1.4 copy-start.7
  182.6 73.9 %copy-start.4 = (bf16[192,2560]{1,0:T(8,128)(2,1)}, bf16[192,2560]{1,0:T(8,128)(2,1)S(1)}, u32[]{:S(2)}) copy-start(bf16[192,2560]{1,0:T(8,128)(2,1)S(1)} %collective-permute-done.2.other_second) | copy-start | bytes 2949124
  256.5 13.7 %collective-permute-start.3 = (bf16[1024,2560]{1,0:T(8,128)(2,1)}, bf16[1024,2560]{1,0:T(8,128)(2,1)}, u32[]{:S(2)}, u32[]{:S(2)}) collective-permute-start(bf16[1024,2560]{1,0:T(8,128)(2,1)} %bitcast.19.rows), channel_id=1, source_target_pairs={{0,8},{8,0},{1,9},{9,1},{2,10},{10,2},{3,11},{11,3},{4,12},{12,4},... | collective-permute-start | bytes 15728648 | tf_op jit(solution)/shard_map/ppermute | solution.py:315
  288.6 12.2 %collective-permute-start.4 = (bf16[1024,2560]{1,0:T(8,128)(2,1)}, bf16[1024,2560]{1,0:T(8,128)(2,1)}, u32[]{:S(2)}, u32[]{:S(2)}) collective-permute-start(bf16[1024,2560]{1,0:T(8,128)(2,1)} %shard_map.134), channel_id=1, source_target_pairs={{0,8},{8,0},{1,9},{9,1},{2,10},{10,2},{3,11},{11,3},{4,12},{12,4},... | collective-permute-start | bytes 15728648 | tf_op jit(solution)/shard_map/ppermute | solution.py:322
  308.5 5.8 %copy-start.8 = (f32[128,6]{0,1:T(8,128)S(1)}, f32[128,6]{0,1:T(8,128)}, u32[]{:S(2)}) copy-start(f32[128,6]{0,1:T(8,128)} %param.19) | copy-start | bytes 9220
  308.5 76.2 %all-to-all-start.3 = ((bf16[64,16,2560]{2,1,0:T(8,128)(2,1)}), bf16[64,16,2560]{2,1,0:T(8,128)(2,1)}, u32[]{:S(2)}, u32[]{:S(2)}) async-start(bf16[64,16,2560]{2,1,0:T(8,128)(2,1)} %bitcast.67), calls=%async_computation.3 | async-start | bytes 10485760 | tf_op jit(solution)/shard_map/all_to_all | solution.py:325
  389.8 17.4 %all-to-all-start.4 = ((bf16[8,16,2560]{2,1,0:T(8,128)(2,1)}), bf16[8,16,2560]{2,1,0:T(8,128)(2,1)S(1)}, u32[]{:S(2)}, u32[]{:S(2)}) async-start(bf16[8,16,2560]{2,1,0:T(8,128)(2,1)} %bitcast.23), calls=%async_computation.4 | async-start | bytes 1310720 | tf_op jit(solution)/shard_map/all_to_all | solution.py:332
Sparse Core Ops, SparseCore 0:
  35.1 105.0 all-gather.1

commit v6 on v3

--- a/solution.py
+++ b/solution.py
@@ -190,7 +190,7 @@
         ),
         input_output_aliases={} if filled is None else {7: 0},
         compiler_params=pltpu.CompilerParams(
-            dimension_semantics=("arbitrary",), vmem_limit_bytes=60 << 20
+            dimension_semantics=("arbitrary",), vmem_limit_bytes=54 << 20
         ),
         cost_estimate=pl.CostEstimate(
             flops=2 * tiles * ROW_TILE * (own_up.size + own_down.size),

time: 416 us -> 413 us (level)
  no operation moved by 1% of the time
where the time goes in v6:
time: 413 us; the launch traced here: 412 us
  waiting for transfers between devices  209 us (51%)
  blocking collectives  70.5 us (17%)
  Pallas kernels  48.3 us (12%)
  starting transfers between devices  31.6 us (8%)
  matrix products  18.4 us (4%)
  between operations  14.5 us (4%)
  other arithmetic  11.2 us (3%)
  local copies, waits for them, and re-layouts  8.85 us (2%)
    ppermute x1, waiting for transfers between devices, per_device(): other_up = lax.ppermute(sent_up, ALL, pairs)  82.5 us
    all_to_all x1, blocking collectives, per_device(): lax.all_to_all(outgoing.reshape(CHIP_COUNT, MOST, model_width), CHIPS, 0,...  70.5 us
    all_to_all x1, waiting for transfers between devices, per_device(): lax.all_to_all(expert_out.reshape(CHIP_COUNT, MOST, model_width), CHIPS,...  68.9 us
    pallas_call x3, Pallas kernels, expert_half(): pl.pallas_call(expert_kernel, out_shape=jax.ShapeDtypeStruct(rows.shape,...  42 us
    all_gather x1, waiting for transfers between devices, per_device(): full_out = lax.all_gather(out_rows, DP, axis=0, tiled=True)  15.3 us
    ppermute x1, waiting for transfers between devices, per_device(): other_first = lax.ppermute(sent_first, ALL, pairs)  14.2 us
    all_to_all x1, waiting for transfers between devices, spread(): lax.all_to_all(jnp.broadcast_to(shard[None], (count,) + shard.shape), axe...  12.8 us
    all_to_all x1, waiting for transfers between devices, per_device(): lax.all_to_all(finished.reshape(cache_size, deal_rows, model_width), CACH...  10.2 us
  transfers between devices with their start and end apart: 11, of which 7 were waited for; matrix products, arithmetic and copies ran while one was open for 5% of the time, Pallas kernels for 7%

profile of v6, /device:TPU:1, one launch (start us, length us, event | category | flops | bytes accessed | tf_op | source)
XLA Modules:
  0.0 412.5 jit_solution(15850457670193023399)
XLA Ops:
  10.1 5.9 %all-to-all-start = ((bf16[8,20,3072]{2,1,0:T(8,128)(2,1)}), bf16[8,20,3072]{2,1,0:T(8,128)(2,1)S(1)}, u32[]{:S(2)}, u32[]{:S(2)}) async-start(bf16[8,20,3072]{2,1,0:T(8,128)(2,1)} %broadcast_in_dim.38), calls=%async_computation | async-start | bytes 2359296 | tf_op jit(solution)/shard_map/all_to_all | solution.py:106
  16.0 4.4 %slice_bitcast_fusion = (bf16[384,2560]{1,0:T(8,128)(2,1)}, bf16[384,2560]{1,0:T(8,128)(2,1)}) fusion(bf16[1,768,2560]{2,1,0:T(8,128)(2,1)} %param.21), kind=kLoop, calls=%fused_computation.10 | loop fusion | bytes 7864320 | tf_op jit(solution)/shard_map/squeeze | solution.py:287
  20.4 12.8 %all-to-all-done = bf16[8,20,3072]{2,1,0:T(8,128)(2,1)S(1)} async-done(((bf16[8,20,3072]{2,1,0:T(8,128)(2,1)}), bf16[8,20,3072]{2,1,0:T(8,128)(2,1)S(1)}, u32[]{:S(2)}, u32[]{:S(2)}) %all-to-all-start) | async-done | bytes 983072 | tf_op jit(solution)/shard_map/all_to_all | solution.py:106
  36.2 3.2 collective-permute-start
  43.2 82.5 %collective-permute-done.other_up = bf16[2560,1536]{1,0:T(8,128)(2,1)} collective-permute-done((bf16[2560,1536]{1,0:T(8,128)(2,1)}, bf16[2560,1536]{1,0:T(8,128)(2,1)}, u32[]{:S(2)}, u32[]{:S(2)}) %collective-permute-start) | collective-permute-done | bytes 7864352 | tf_op jit(solution)/shard_map/ppermute | solution.py:240
  125.6 3.0 fusion.4.projected
  130.8 3.6 all-to-all-start.1
  134.4 4.0 fusion.projected
  138.4 14.2 %collective-permute-done.1.other_first = bf16[384,2560]{1,0:T(8,128)(2,1)} collective-permute-done((bf16[384,2560]{1,0:T(8,128)(2,1)}, bf16[384,2560]{1,0:T(8,128)(2,1)}, u32[]{:S(2)}, u32[]{:S(2)}) %collective-permute-start.1) | collective-permute-done | bytes 1966112 | tf_op jit(solution)/shard_map/ppermute | solution.py:241
  152.6 4.5 %all-to-all-done.1 = bf16[8,128,512]{2,1,0:T(8,128)(2,1)S(1)} async-done(((bf16[8,128,512]{2,1,0:T(8,128)(2,1)}), bf16[8,128,512]{2,1,0:T(8,128)(2,1)S(1)}, u32[]{:S(2)}, u32[]{:S(2)}) %all-to-all-start.1) | async-done | bytes 1048608 | tf_op jit(solution)/shard_map/all_to_all | solution.py:284
  157.1 4.4 %collective-permute-start.2 = (bf16[384,2560]{1,0:T(8,128)(2,1)}, bf16[384,2560]{1,0:T(8,128)(2,1)}, u32[]{:S(2)}, u32[]{:S(2)}) collective-permute-start(bf16[384,2560]{1,0:T(8,128)(2,1)} %get-tuple-element.24), channel_id=1, source_target_pairs={{8,1},{1,8},{10,3},{3,10},{12,5},{5,12},{14,7},{7,14},{24,17},{17,... | collective-permute-start | bytes 5898248 | tf_op jit(solution)/shard_map/ppermute | solution.py:289
  162.3 4.1 shard_map.131
  166.4 15.3 %all-gather.5.cloned.1.call-done = bf16[1280,2560]{1,0:T(8,128)(2,1)} async-done(((bf16[80,2560]{1,0:T(8,128)(2,1)}), bf16[1280,2560]{1,0:T(8,128)(2,1)}) %all-gather.5.cloned.1.call-update) | async-done | bytes 6553616 | tf_op jit(solution)/shard_map/all_gather | solution.py:245
  181.7 4.0 multiply_reduce_fusion
  187.4 70.5 %all_to_all.25 = bf16[64,16,2560]{2,1,0:T(8,128)(2,1)} all-to-all(bf16[64,16,2560]{2,1,0:T(8,128)(2,1)S(1)} %bitcast.50), channel_id=1, replica_groups=mesh['yh'=2,'z'=4,'core'=2,'yl'=2,'x'=4] {'yh','z','yl','x'}, dimensions={0} | all-to-all | bytes 10485760 | tf_op jit(solution)/shard_map/all_to_all | solution.py:299
  259.6 11.8 %shard_map.132.rest_0_ = bf16[1024,2560]{1,0:T(8,128)(2,1)} custom-call(s32[1]{0:T(128)} %bitcast.13.keep, bf16[1024,2560]{1,0:T(8,128)(2,1)} %bitcast.15.rows, bf16[2560,1536]{1,0:T(8,128)(2,1)} %bitcast.55, bf16[2560,1536]{1,0:T(8,128)(2,1)} %collective-permute-done.other_up, bf16[768,2560]{1,0:T(8,128)(2,1)} %bitcast.51, ...), custom_call_target="tpu_custom_call" | custom-call | flops 6039797760 | bytes 17039360 | tf_op jit(solution)/shard_map/pallas_call | solution.py:176
  271.5 18.3 %shard_map.134 = bf16[1024,2560]{1,0:T(8,128)(2,1)} custom-call(s32[1]{0:T(128)} %bitcast.13.keep, bf16[1024,2560]{1,0:T(8,128)(2,1)} %collective-permute-done.3.rows, bf16[2560,1536]{1,0:T(8,128)(2,1)} %bitcast.56, bf16[2560,1536]{1,0:T(8,128)(2,1)} %collective-permute-done.other_up, bf16[768,2560]{1,0:T(8,128)(2,1)} %bitcast.52, ...), custom_call_target="tpu_custom_call" | custom-call | flops 12079595520 | bytes 22282240 | tf_op jit(solution)/shard_map/pallas_call | solution.py:176
  290.1 11.8 %shard_map.133 = bf16[1024,2560]{1,0:T(8,128)(2,1)} custom-call(s32[1]{0:T(128)} %bitcast.13.keep, bf16[1024,2560]{1,0:T(8,128)(2,1)} %bitcast.15.rows, bf16[2560,1536]{1,0:T(8,128)(2,1)} %bitcast.57, bf16[2560,1536]{1,0:T(8,128)(2,1)} %collective-permute-done.other_up, bf16[768,2560]{1,0:T(8,128)(2,1)} %bitcast.53, ...), custom_call_target="tpu_custom_call", output_to_operand_aliasing={{}: (7, {})} | custom-call | flops 6039797760 | bytes 17039360 | tf_op jit(solution)/shard_map/pallas_call | solution.py:176
  302.0 6.5 %add_convert_fusion = bf16[1024,2560]{1,0:T(8,128)(2,1)} fusion(bf16[1024,2560]{1,0:T(8,128)(2,1)S(1)} %collective-permute-done.4, bf16[1024,2560]{1,0:T(8,128)(2,1)} %shard_map.133), kind=kLoop, calls=%fused_computation | loop fusion | flops 10485760 | bytes 15728640 | tf_op jit(solution)/shard_map/convert_element_type | solution.py:311
  308.5 5.8 %all-to-all-start.3 = ((bf16[64,16,2560]{2,1,0:T(8,128)(2,1)}), bf16[64,16,2560]{2,1,0:T(8,128)(2,1)}, u32[]{:S(2)}, u32[]{:S(2)}) async-start(bf16[64,16,2560]{2,1,0:T(8,128)(2,1)} %bitcast.58), calls=%async_computation.3 | async-start | bytes 10485760 | tf_op jit(solution)/shard_map/all_to_all | solution.py:312
  314.6 68.9 %all-to-all-done.3 = bf16[64,16,2560]{2,1,0:T(8,128)(2,1)} async-done(((bf16[64,16,2560]{2,1,0:T(8,128)(2,1)}), bf16[64,16,2560]{2,1,0:T(8,128)(2,1)}, u32[]{:S(2)}, u32[]{:S(2)}) %all-to-all-start.3) | async-done | bytes 5242912 | tf_op jit(solution)/shard_map/all_to_all | solution.py:312
  383.6 4.2 %fusion.15 = f32[256,2560]{1,0:T(8,128)S(1)} fusion(bf16[1024,2560]{1,0:T(8,128)(2,1)} %bitcast.18, bf16[1024,128]{1,0:T(8,128)(2,1)S(1)} %get-tuple-element.40, bf16[1024,128]{1,0:T(8,128)(2,1)S(1)} %get-tuple-element.39), kind=kOutput, calls=%fused_computation.30 | convolution fusion | flops 1343225856 | bytes 8388608 | tf_op jit(solution)/shard_map/dot_general | solution.py:315
  388.8 4.3 %all-to-all-start.4 = ((bf16[8,16,2560]{2,1,0:T(8,128)(2,1)}), bf16[8,16,2560]{2,1,0:T(8,128)(2,1)S(1)}, u32[]{:S(2)}, u32[]{:S(2)}) async-start(bf16[8,16,2560]{2,1,0:T(8,128)(2,1)} %bitcast.19), calls=%async_computation.4 | async-start | bytes 1310720 | tf_op jit(solution)/shard_map/all_to_all | solution.py:321
  394.2 10.2 %all-to-all-done.4 = bf16[8,16,2560]{2,1,0:T(8,128)(2,1)S(1)} async-done(((bf16[8,16,2560]{2,1,0:T(8,128)(2,1)}), bf16[8,16,2560]{2,1,0:T(8,128)(2,1)S(1)}, u32[]{:S(2)}, u32[]{:S(2)}) %all-to-all-start.4) | async-done | bytes 655392 | tf_op jit(solution)/shard_map/all_to_all | solution.py:321
  (72 shorter events, 19.7 us)
Async XLA Ops:
  10.1 23.1 %all-to-all-start = ((bf16[8,20,3072]{2,1,0:T(8,128)(2,1)}), bf16[8,20,3072]{2,1,0:T(8,128)(2,1)S(1)}, u32[]{:S(2)}, u32[]{:S(2)}) async-start(bf16[8,20,3072]{2,1,0:T(8,128)(2,1)} %broadcast_in_dim.38), calls=%async_computation | async-start | bytes 2359296 | tf_op jit(solution)/shard_map/all_to_all | solution.py:106
  15.9 109.7 %all-gather.3.cloned.1.call-start = ((), (), s32[]{:S(2)}) async-start(), calls=%async_computation.5 | async-start | bytes 9748480 | tf_op jit(solution)/shard_map/all_gather | solution.py:244
  34.2 5.2 %copy-start.2 = (s32[1024]{0:T(1024)S(1)}, s32[1024]{0:T(1024)}, u32[]{:S(2)}) copy-start(s32[1024]{0:T(1024)} %param.12) | copy-start | bytes 12292
  34.2 5.2 %copy-start.9 = (s32[128]{0:T(128)S(1)}, s32[128]{0:T(128)}, u32[]{:S(2)}) copy-start(s32[128]{0:T(128)} %param.13) | copy-start | bytes 1540
  34.3 8.7 %copy-start.5 = (bf16[128,2560]{1,0:T(8,128)(2,1)S(1)}, bf16[128,2560]{1,0:T(8,128)(2,1)}, u32[]{:S(2)}) copy-start(bf16[128,2560]{1,0:T(8,128)(2,1)} %param.11) | copy-start | bytes 1966084
  34.3 91.3 %copy-start.10 = (f32[2560]{0:T(1024)S(1)}, f32[2560]{0:T(1024)}, u32[]{:S(2)}) copy-start(f32[2560]{0:T(1024)} %param.14) | copy-start | bytes 30724
  35.4 146.3 %all-gather.5.cloned.1.call-start = ((), (), s32[]{:S(2)}) async-start(), calls=%async_computation.6 | async-start | bytes 6963200 | tf_op jit(solution)/shard_map/all_gather | solution.py:245
  36.2 89.5 %collective-permute-start = (bf16[2560,1536]{1,0:T(8,128)(2,1)}, bf16[2560,1536]{1,0:T(8,128)(2,1)}, u32[]{:S(2)}, u32[]{:S(2)}) collective-permute-start(bf16[2560,1536]{1,0:T(8,128)(2,1)} %bitcast.54), channel_id=1, source_target_pairs={{8,1},{1,8},{10,3},{3,10},{12,5},{5,12},{14,7},{7,14},{24,17},{17,... | collective-permute-start | bytes 23592968 | tf_op jit(solution)/shard_map/ppermute | solution.py:240
  39.5 113.1 %collective-permute-start.1 = (bf16[384,2560]{1,0:T(8,128)(2,1)}, bf16[384,2560]{1,0:T(8,128)(2,1)}, u32[]{:S(2)}, u32[]{:S(2)}) collective-permute-start(bf16[384,2560]{1,0:T(8,128)(2,1)} %get-tuple-element.20), channel_id=1, source_target_pairs={{8,1},{1,8},{10,3},{3,10},{12,5},{5,12},{14,7},{7,14},{24,17},{17,... | collective-permute-start | bytes 5898248 | tf_op jit(solution)/shard_map/ppermute | solution.py:241
  130.8 26.3 %all-to-all-start.1 = ((bf16[8,128,512]{2,1,0:T(8,128)(2,1)}), bf16[8,128,512]{2,1,0:T(8,128)(2,1)S(1)}, u32[]{:S(2)}, u32[]{:S(2)}) async-start(bf16[8,128,512]{2,1,0:T(8,128)(2,1)} %shard_map.130), calls=%async_computation.1 | async-start | bytes 2097152 | tf_op jit(solution)/shard_map/all_to_all | solution.py:284
  134.4 27.5 %copy-start.8 = (s32[128,6]{0,1:T(8,128)S(1)}, s32[128,6]{0,1:T(8,128)}, u32[]{:S(2)}) copy-start(s32[128,6]{0,1:T(8,128)} %param.18) | copy-start | bytes 9220
  134.4 27.9 %copy-start = (f32[128,128]{1,0:T(8,128)S(1)}, f32[128,128]{1,0:T(8,128)}, u32[]{:S(2)}) copy-start(f32[128,128]{1,0:T(8,128)} %get-tuple-element.48.cosines) | copy-start | bytes 196612
  134.4 27.9 %copy-start.1 = (f32[128,128]{1,0:T(8,128)S(1)}, f32[128,128]{1,0:T(8,128)}, u32[]{:S(2)}) copy-start(f32[128,128]{1,0:T(8,128)} %get-tuple-element.49.sines) | copy-start | bytes 196612
  157.1 30.2 %collective-permute-start.2 = (bf16[384,2560]{1,0:T(8,128)(2,1)}, bf16[384,2560]{1,0:T(8,128)(2,1)}, u32[]{:S(2)}, u32[]{:S(2)}) collective-permute-start(bf16[384,2560]{1,0:T(8,128)(2,1)} %get-tuple-element.24), channel_id=1, source_target_pairs={{8,1},{1,8},{10,3},{3,10},{12,5},{5,12},{14,7},{7,14},{24,17},{17,... | collective-permute-start | bytes 5898248 | tf_op jit(solution)/shard_map/ppermute | solution.py:289
  166.4 19.3 %copy-start.6 = (f32[2560]{0:T(1024)S(1)}, f32[2560]{0:T(1024)}, u32[]{:S(2)}) copy-start(f32[2560]{0:T(1024)} %param.17) | copy-start | bytes 30724
  185.7 1.6 copy-start.3
  257.9 13.6 %collective-permute-start.3 = (bf16[1024,2560]{1,0:T(8,128)(2,1)}, bf16[1024,2560]{1,0:T(8,128)(2,1)}, u32[]{:S(2)}, u32[]{:S(2)}) collective-permute-start(bf16[1024,2560]{1,0:T(8,128)(2,1)} %bitcast.15.rows), channel_id=1, source_target_pairs={{0,8},{8,0},{1,9},{9,1},{2,10},{10,2},{3,11},{11,3},{4,12},{12,4},... | collective-permute-start | bytes 15728648 | tf_op jit(solution)/shard_map/ppermute | solution.py:302
  289.8 12.2 %collective-permute-start.4 = (bf16[1024,2560]{1,0:T(8,128)(2,1)}, bf16[1024,2560]{1,0:T(8,128)(2,1)S(1)}, u32[]{:S(2)}, u32[]{:S(2)}) collective-permute-start(bf16[1024,2560]{1,0:T(8,128)(2,1)} %shard_map.134), channel_id=1, source_target_pairs={{0,8},{8,0},{1,9},{9,1},{2,10},{10,2},{3,11},{11,3},{4,12},{12,4},... | collective-permute-start | bytes 15728648 | tf_op jit(solution)/shard_map/ppermute | solution.py:309
  308.5 5.8 %copy-start.7 = (f32[128,6]{0,1:T(8,128)S(1)}, f32[128,6]{0,1:T(8,128)}, u32[]{:S(2)}) copy-start(f32[128,6]{0,1:T(8,128)} %param.19) | copy-start | bytes 9220
  308.5 75.0 %all-to-all-start.3 = ((bf16[64,16,2560]{2,1,0:T(8,128)(2,1)}), bf16[64,16,2560]{2,1,0:T(8,128)(2,1)}, u32[]{:S(2)}, u32[]{:S(2)}) async-start(bf16[64,16,2560]{2,1,0:T(8,128)(2,1)} %bitcast.58), calls=%async_computation.3 | async-start | bytes 10485760 | tf_op jit(solution)/shard_map/all_to_all | solution.py:312
  383.6 4.2 %copy-start.4 = (f32[128,2560]{1,0:T(8,128)S(1)}, f32[128,2560]{1,0:T(8,128)}, u32[]{:S(2)}) copy-start(f32[128,2560]{1,0:T(8,128)} %copy-done.3) | copy-start | bytes 3932164
  388.8 15.7 %all-to-all-start.4 = ((bf16[8,16,2560]{2,1,0:T(8,128)(2,1)}), bf16[8,16,2560]{2,1,0:T(8,128)(2,1)S(1)}, u32[]{:S(2)}, u32[]{:S(2)}) async-start(bf16[8,16,2560]{2,1,0:T(8,128)(2,1)} %bitcast.19), calls=%async_computation.4 | async-start | bytes 1310720 | tf_op jit(solution)/shard_map/all_to_all | solution.py:321
Sparse Core Ops, SparseCore 0:
  35.5 76.9 all-gather.2
  115.0 66.6 all-gather.4
